TPU v7x, 512 devices: a whole 4x4x16 slice. The times are simulated.
512 devices in a mesh: row: 32 (over x, z_lo, core), col: 16 (over y, z_hi).
Axes of the slice: x: 4, y: 4, z: 16 (z_hi: 4, z_lo: 4; z = z_hi * 4 + z_lo), core: 2. Of those that a mesh axis runs over, the one named last changes fastest.
Arguments:
- features: bfloat16 [65536, 128], P(('row', 'col')), may hold values from -6 to 6
- weight: bfloat16 [128, 128], replicated, may hold values from -0.5 to 0.5
- adj_values: bfloat16 [32, 16, 16, 128, 128], P('row', 'col'), may hold values from -0.125 to 0.125
- tile_rows: int32 [32, 16, 16], P('row', 'col'), may hold values from 0 to 15
- tile_cols: int32 [32, 16, 16], P('row', 'col'), may hold values from 0 to 31
- cotangent: bfloat16 [65536, 128], P(('row', 'col')), may hold values from -6 to 6
Outputs:
- activations: float32 [65536, 128], P(('row', 'col'))
- grad_features: float32 [65536, 128], P(('row', 'col'))
- grad_weight: float32 [128, 128], replicated
All inputs are finite; a program needn't handle non-finite values.
Results may differ from a plain program's by a relative error of at most 0.0049.
Values may be sent and summed in bfloat16 or wider, within the bound.
No kernel may reach another device: no remote copies, remote signals or barrier semaphores. Data moves between devices by JAX's collectives and lax.ppermute only.
A program may use at most 64 MiB of HBM per device.

v0:
```python
import jax
import jax.numpy as jnp
from jax import lax
from jax.sharding import PartitionSpec as P


def per_device(features, weight, adj_values, tile_rows, tile_cols, cotangent):
    blocks = adj_values[0, 0]
    rows_id = tile_rows[0, 0]
    cols_id = tile_cols[0, 0]
    tile = blocks.shape[-1]
    owned = features.shape[0]
    width = features.shape[1]
    n_row = lax.axis_size("row")
    n_col = lax.axis_size("col")
    col_block = lax.all_gather(features, "row", axis=0, tiled=True)
    picked = col_block.reshape(-1, tile, width)[cols_id]
    prods = jnp.einsum("tab,tbf->taf", blocks, picked, preferred_element_type=jnp.float32)
    partial_rows = jax.ops.segment_sum(prods, rows_id, num_segments=n_col * owned // tile)
    aggregated = lax.psum_scatter(
        partial_rows.reshape(-1, width), "col", scatter_dimension=0, tiled=True
    )
    zed = aggregated.astype(jnp.bfloat16)
    pre = jnp.dot(zed, weight, preferred_element_type=jnp.float32)
    sig = jax.nn.sigmoid(pre)
    activations = pre * sig
    dpre = (cotangent.astype(jnp.float32) * sig * (1.0 + pre * (1.0 - sig))).astype(jnp.bfloat16)
    weight_part = lax.dot_general(
        zed, dpre, (((0,), (0,)), ((), ())), preferred_element_type=jnp.float32
    )
    grad_weight = lax.psum(weight_part, ("row", "col"))
    dzed = lax.dot_general(
        dpre, weight, (((1,), (1,)), ((), ())), preferred_element_type=jnp.float32
    ).astype(jnp.bfloat16)
    row_block = lax.all_gather(dzed, "col", axis=0, tiled=True)
    picked_back = row_block.reshape(-1, tile, width)[rows_id]
    prods_back = jnp.einsum("tab,taf->tbf", blocks, picked_back, preferred_element_type=jnp.float32)
    partial_cols = jax.ops.segment_sum(prods_back, cols_id, num_segments=n_row * owned // tile)
    grad_features = lax.psum_scatter(
        partial_cols.reshape(-1, width), "row", scatter_dimension=0, tiled=True
    )
    return (activations, grad_features, grad_weight)


def solution(mesh):
    return jax.shard_map(
        per_device,
        mesh=mesh,
        in_specs=(
            P(("row", "col"), None),
            P(),
            P("row", "col", None, None, None),
            P("row", "col", None),
            P("row", "col", None),
            P(("row", "col"), None),
        ),
        out_specs=(P(("row", "col"), None), P(("row", "col"), None), P()),
        check_vma=False,
    )
```

profile of v0, /device:TPU:1, one launch (start us, length us, event | category | flops | bytes accessed | tf_op | source)
XLA Modules:
  0.0 802.0 jit_solution(2386239688956795602)
XLA Ops:
  7.2 0.0 copy-start
  7.2 0.0 all-gather.2.cloned.1.call-start
  7.2 0.7 all-gather.2.cloned.1.call-update
  7.9 0.0 reduce-scatter.3.cloned.1.call-start
  8.0 0.7 fusion.7
  8.6 71.0 %all-gather.2.cloned.1.call-done = bf16[4096,128]{1,0:T(8,128)(2,1)} async-done(((bf16[128,128]{1,0:T(8,128)(2,1)}), bf16[4096,128]{1,0:T(8,128)(2,1)}) %all-gather.2.cloned.1.call-update) | async-done | bytes 1048592 | tf_op jit(solution)/shard_map/all_gather | solution.py:16
  79.7 1.9 gather_fusion
  81.5 0.0 copy-done
  81.5 0.5 convolution_bitcast_fusion.1
  82.1 0.0 copy-start.4
  82.1 0.3 copy.12
  82.4 0.1 broadcast_in_dim.8
  82.5 0.2 copy-done.4
  82.7 0.0 copy-start.3
  82.7 0.0 copy-start.6
  82.7 1.6 scatter_fusion
  84.3 0.0 copy-start.2
  84.3 1.0 copy-done.2
  85.3 0.0 reduce-scatter.3.cloned.1.call-update
  85.3 0.0 all-reduce.2.cloned.1.call-start
  85.4 112.6 %reduce-scatter.3.cloned.1.call-done = f32[128,128]{1,0:T(8,128)} async-done(((f32[2048,128]{1,0:T(8,128)}), f32[128,128]{1,0:T(8,128)}) %reduce-scatter.3.cloned.1.call-update) | async-done | bytes 65552 | tf_op jit(solution)/shard_map/reduce_scatter | solution.py:20
  198.0 0.0 copy-done.3
  198.0 0.0 copy-done.6
  198.0 1.6 multiply_convert_fusion
  199.7 0.1 convolution_convert_fusion
  199.8 1.7 fusion.3
  201.5 0.0 all-reduce.2.cloned.1.call-update
  201.5 0.0 reduce-scatter.5.cloned.1.call-start
  201.6 49.3 %all_gather.7 = bf16[2048,128]{1,0:T(8,128)(2,1)S(1)} all-gather(bf16[128,128]{1,0:T(8,128)(2,1)S(1)} %convolution_convert_fusion), channel_id=1, replica_groups=mesh['row'=32,'col'=16] {'col'}, dimensions={0}, use_global_device_ids=true | all-gather | bytes 557056 | tf_op jit(solution)/shard_map/all_gather | solution.py:35
  250.8 0.6 gather_fusion.1
  251.5 0.3 convolution_bitcast_fusion
  251.8 0.0 copy-start.5
  251.9 1.3 copy.14
  253.2 0.2 broadcast_in_dim.9
  253.4 0.0 copy-done.5
  253.4 2.6 scatter_fusion.1
  256.0 0.0 copy-start.1
  256.0 1.3 copy-done.1
  257.4 0.0 reduce-scatter.5.cloned.1.call-update
  257.4 392.5 %all-reduce.2.cloned.1.call-done = f32[128,128]{1,0:T(8,128)} async-done(((f32[128,128]{1,0:T(8,128)}), f32[128,128]{1,0:T(8,128)}) %all-reduce.2.cloned.1.call-update) | async-done | bytes 65552 | tf_op jit(solution)/shard_map/psum | solution.py:31
  649.9 144.1 %reduce-scatter.5.cloned.1.call-done = f32[128,128]{1,0:T(8,128)} async-done(((f32[4096,128]{1,0:T(8,128)}), f32[128,128]{1,0:T(8,128)}) %reduce-scatter.5.cloned.1.call-update) | async-done | bytes 65552 | tf_op jit(solution)/shard_map/reduce_scatter | solution.py:39
  794.0 1.5 copy.20
  (3 shorter events, 0.0 us)
Async XLA Ops:
  7.2 74.4 %copy-start = (bf16[1,1,16,128,128]{4,3,2,1,0:T(8,128)(2,1)S(1)}, bf16[1,1,16,128,128]{4,3,2,1,0:T(8,128)(2,1)}, u32[]{:S(2)}) copy-start(bf16[1,1,16,128,128]{4,3,2,1,0:T(8,128)(2,1)} %param.8) | copy-start | bytes 1572868
  7.2 72.5 %all-gather.2.cloned.1.call-start = ((), (), s32[]{:S(2)}) async-start(), calls=%async_computation.2 | async-start | bytes 1081344 | tf_op jit(solution)/shard_map/all_gather | solution.py:16
  7.9 190.1 %reduce-scatter.3.cloned.1.call-start = ((), (), s32[]{:S(2)}) async-start(), calls=%async_computation.3 | async-start | bytes 1114112 | tf_op jit(solution)/shard_map/reduce_scatter | solution.py:20
  82.1 0.7 copy-start.4
  82.7 115.3 %copy-start.3 = (bf16[128,128]{1,0:T(8,128)(2,1)S(1)}, bf16[128,128]{1,0:T(8,128)(2,1)}, u32[]{:S(2)}) copy-start(bf16[128,128]{1,0:T(8,128)(2,1)} %param.7) | copy-start | bytes 98308
  82.7 115.3 %copy-start.6 = (bf16[128,128]{1,0:T(8,128)(2,1)S(1)}, bf16[128,128]{1,0:T(8,128)(2,1)}, u32[]{:S(2)}) copy-start(bf16[128,128]{1,0:T(8,128)(2,1)} %param.11) | copy-start | bytes 98308
  84.3 1.0 copy-start.2
  85.3 564.5 %all-reduce.2.cloned.1.call-start = ((), (), s32[]{:S(2)}) async-start(), calls=%async_computation.5 | async-start | bytes 131072 | tf_op jit(solution)/shard_map/psum | solution.py:31
  201.5 592.5 %reduce-scatter.5.cloned.1.call-start = ((), (), s32[]{:S(2)}) async-start(), calls=%async_computation.4 | async-start | bytes 2162688 | tf_op jit(solution)/shard_map/reduce_scatter | solution.py:39
  251.8 1.6 copy-start.5
  256.0 1.3 copy-start.1
Sparse Core Ops, SparseCore 0:
  10.1 69.4 all-gather.1
  85.4 112.5 reduce-scatter.2
  204.1 445.7 all-reduce.1
  653.1 140.8 reduce-scatter.4
where the time goes:
time: 806 us; the launch traced here: 802 us
  waiting for transfers between devices  721 us (89%)
  blocking collectives  49.3 us (6%)
  between operations  13.9 us (2%)
  local copies, waits for them, and re-layouts  8.49 us (1%)
    psum x1, waiting for transfers between devices, per_device(): grad_weight = lax.psum(weight_part, ('row', 'col'))  392 us
    reduce_scatter x1, waiting for transfers between devices, per_device(): lax.psum_scatter(partial_cols.reshape(-1, width), 'row', scatter_dimensio...  144 us
    reduce_scatter x1, waiting for transfers between devices, per_device(): lax.psum_scatter(partial_rows.reshape(-1, width), 'col', scatter_dimensio...  113 us
    all_gather x1, waiting for transfers between devices, per_device(): col_block = lax.all_gather(features, 'row', axis=0, tiled=True)  71 us
    all_gather x1, blocking collectives, per_device(): row_block = lax.all_gather(dzed, 'col', axis=0, tiled=True)  49.3 us
  transfers between devices with their start and end apart: 4, of which 4 were waited for; matrix products, arithmetic and copies ran while one was open for 1% of the time, Pallas kernels for 0%

commit v1 on v0

v1 whole, which is shorter than its diff:
```python
import itertools

import jax
import jax.numpy as jnp
from jax import lax
from jax.experimental import pallas as pl
from jax.experimental.pallas import tpu as pltpu
from jax.sharding import PartitionSpec as P

BOTH = ("row", "col")
SIZES = {"x": 4, "zl": 4, "core": 2, "y": 4, "zh": 4}
F = 128
T = 128
BF = jnp.bfloat16
F32 = jnp.float32


def position(place):
    n = 0
    for name, size in SIZES.items():
        n = n * size + place[name]
    return n


def places():
    for values in itertools.product(*(range(s) for s in SIZES.values())):
        yield dict(zip(SIZES, values))


def groups(axis):
    found = {}
    for place in places():
        key = tuple(v for n, v in place.items() if n != axis)
        found.setdefault(key, []).append(position(place))
    return list(found.values())


def swap_core(array):
    pairs = [(position(p), position({**p, "core": 1 - p["core"]})) for p in places()]
    return lax.ppermute(array, BOTH, pairs)


def gather(array, axis):
    return lax.all_gather(array, BOTH, axis=0, tiled=False, axis_index_groups=groups(axis))


def exchange(array, axis):
    return lax.all_to_all(array, BOTH, 0, 0, tiled=True, axis_index_groups=groups(axis))


def dot(a, b, dims):
    return lax.dot_general(a, b, (dims, ((), ())), preferred_element_type=F32)


def call(body, outs, spaces, scratch=()):
    kinds = {"v": pltpu.VMEM, "s": pltpu.SMEM}
    return pl.pallas_call(
        body,
        out_shape=[jax.ShapeDtypeStruct(s, d) for s, d in outs],
        in_specs=[pl.BlockSpec(memory_space=kinds[k]) for k in spaces],
        out_specs=[pl.BlockSpec(memory_space=pltpu.VMEM) for _ in outs],
        scratch_shapes=list(scratch),
    )


def forward_tiles(rows, cols, adj, own, other, out, acc):
    core = lax.rem(lax.axis_index("row"), 2)
    acc[...] = jnp.zeros_like(acc)
    for t in range(16):
        b = cols[t]
        spot = lax.div(b, 2)
        mine = lax.rem(b, 2) == core
        x = jnp.where(mine, own[spot], other[spot])
        r = rows[t]
        acc[r] += dot(adj[t], x, ((1,), (0,)))
    out[...] = acc[...].astype(BF)


def sum_rows(parts, cot, out):
    total = parts[0].astype(F32)
    for k in range(1, 4):
        total += parts[k].astype(F32)
    out[pl.ds(0, 512), :] = total.astype(BF)
    out[pl.ds(512, 128), :] = cot[...]


def layer(parts, weight, act, out, kept):
    total = parts[0, pl.ds(0, 512), :].astype(F32)
    for k in range(1, 4):
        total += parts[k, pl.ds(0, 512), :].astype(F32)
    zed = total.astype(BF)
    w = weight[...]
    pre = dot(zed, w, ((1,), (0,)))
    sig = jax.nn.sigmoid(pre)
    kept[...] = (pre * sig).reshape(4, T, F)
    act[...] = kept[lax.rem(lax.axis_index("col"), 4)]
    cot = jnp.concatenate([parts[k, pl.ds(512, 128), :] for k in range(4)], axis=0)
    dpre = (cot.astype(F32) * sig * (1.0 + pre * (1.0 - sig))).astype(BF)
    out[pl.ds(0, 512), :] = dot(dpre, w, ((1,), (1,))).astype(BF)
    grad = dot(zed, dpre, ((0,), (0,)))
    high = grad.astype(BF)
    out[pl.ds(512, 128), :] = high
    out[pl.ds(640, 128), :] = (grad - high.astype(F32)).astype(BF)


def backward_tiles(rows, cols, adj, parts, keep, send, acc):
    core = lax.rem(lax.axis_index("row"), 2)
    acc[...] = jnp.zeros_like(acc)
    for t in range(16):
        r = rows[t]
        b = cols[t]
        start = pl.multiple_of(lax.rem(r, 4) * T, T)
        d = parts[lax.div(r, 4), pl.ds(start, T), :]
        acc[lax.rem(b, 2), lax.div(b, 2)] += dot(adj[t], d, ((0,), (0,)))
    keep[pl.ds(0, 16)] = acc[core]
    send[pl.ds(0, 16)] = acc[1 - core]
    grad = jnp.zeros((F, F), F32)
    for k in range(4):
        grad += parts[k, pl.ds(512, 128), :].astype(F32)
        grad += parts[k, pl.ds(640, 128), :].astype(F32)
    keep[16] = grad
    send[16] = grad


def split(grad):
    high = grad.astype(BF)
    return high, (grad - high.astype(F32)).astype(BF)


def add_cores(keep, got, out):
    high, low = split(keep[16] + got[16])
    for k in range(4):
        tiles = keep[pl.ds(4 * k, 4)] + got[pl.ds(4 * k, 4)]
        out[k, pl.ds(0, 4)] = tiles.astype(BF)
        out[k, 4] = high
        out[k, 5] = low


def add_x(parts, out):
    total = parts[0].astype(F32)
    for k in range(1, 4):
        total += parts[k].astype(F32)
    high, low = split(total[4] + total[5])
    for k in range(4):
        out[k, 0] = total[k].astype(BF)
        out[k, 1] = high
        out[k, 2] = low


def add_z(parts, out, grad):
    total = parts[0].astype(F32)
    for k in range(1, 4):
        total += parts[k].astype(F32)
    out[...] = total[0]
    grad[...] = total[1] + total[2]


def per_device(features, weight, adj_values, tile_rows, tile_cols, cotangent):
    adj = adj_values.reshape(16, T, T)
    rows = tile_rows.reshape(16)
    cols = tile_cols.reshape(16)

    own = gather(gather(features, "zl"), "x").reshape(16, T, F)
    other = swap_core(own)
    (partial,) = call(
        forward_tiles, [((16, T, F), BF)], "ssvvv", [pltpu.VMEM((16, T, F), F32)]
    )(rows, cols, adj, own, other)
    parts = exchange(partial.reshape(4, 512, F), "y")
    (summed,) = call(sum_rows, [((640, F), BF)], "vv")(parts, cotangent)
    parts = gather(summed, "zh")
    act, back = call(
        layer, [((T, F), F32), ((768, F), BF)], "vv", [pltpu.VMEM((4, T, F), F32)]
    )(parts, weight)
    parts = gather(back, "y")
    keep, send = call(
        backward_tiles,
        [((17, T, F), F32), ((17, T, F), F32)],
        "ssvv",
        [pltpu.VMEM((2, 16, T, F), F32)],
    )(rows, cols, adj, parts)
    got = swap_core(send)
    (parts,) = call(add_cores, [((4, 6, T, F), BF)], "vv")(keep, got)
    parts = exchange(parts, "x")
    (parts,) = call(add_x, [((4, 3, T, F), BF)], "v")(parts)
    parts = exchange(parts, "zl")
    out, grad = call(add_z, [((T, F), F32), ((F, F), F32)], "v")(parts)
    return act, out, grad


def solution(mesh):
    return jax.shard_map(
        per_device,
        mesh=mesh,
        in_specs=(
            P(BOTH, None),
            P(),
            P("row", "col", None, None, None),
            P("row", "col", None),
            P("row", "col", None),
            P(BOTH, None),
        ),
        out_specs=(P(BOTH, None), P(BOTH, None), P()),
        check_vma=False,
    )
```

time: 806 us -> 152 us (0.19)
  waiting for transfers between devices: 721 us -> 4.08 us
  blocking collectives: 49.3 us -> 108 us
  starting transfers between devices: 0.16 us -> 21 us
  Pallas kernels: 0 us -> 16 us
  between operations: 13.9 us -> 0.66 us
    psum x1 -> x0, waiting for transfers between devices: 392 us -> none  [per_device(): grad_weight = lax.psum(weight_part, ('row', 'col'))]
    reduce_scatter x2 -> x0, waiting for transfers between devices: 257 us -> none  [the longest x1 144 us: per_device(): lax.psum_scatter(partial_cols.reshape(-1, width), 'row', scatter_dimensio...]
    all_gather x1 -> x0, waiting for transfers between devices: 71 us -> none  [per_device(): col_block = lax.all_gather(features, 'row', axis=0, tiled=True)]
    all_to_all x0 -> x3, blocking collectives: none -> 44.2 us  [exchange(): lax.all_to_all(array, BOTH, 0, 0, tiled=True, axis_index_groups=groups(ax...]
    ppermute x0 -> x2, starting transfers between devices: none -> 21 us  [swap_core(): return lax.ppermute(array, BOTH, pairs)]
    pallas_call x0 -> x7, Pallas kernels: none -> 16 us  [the longest x1 3.21 us: per_device(): call(backward_tiles, [((17, T, F), F32), ((17, T, F), F32)], 'ssvv', [plt...]
    all_gather x1 -> x4, blocking collectives: 49.3 us -> 63.9 us  [gather(): lax.all_gather(array, BOTH, axis=0, tiled=False, axis_index_groups=groups...]
  transfers between devices with their start and end apart: 4 -> 2, of which waited for: 4 -> 2; matrix products, arithmetic and copies ran while one was open for 1% -> 0% of each run, Pallas kernels for 0% -> 0%
where the time goes in v1:
time: 152 us
  blocking collectives  108 us (71%)
  starting transfers between devices  21 us (14%)
  Pallas kernels  16 us (11%)
  waiting for transfers between devices  4.08 us (3%)
  local copies, waits for them, and re-layouts  1.83 us (1%)
    all_gather x4, blocking collectives, gather(): lax.all_gather(array, BOTH, axis=0, tiled=False, axis_index_groups=groups...  63.9 us
    all_to_all x3, blocking collectives, exchange(): lax.all_to_all(array, BOTH, 0, 0, tiled=True, axis_index_groups=groups(ax...  44.2 us
    ppermute x2, starting transfers between devices, swap_core(): return lax.ppermute(array, BOTH, pairs)  21 us
    ppermute x2, waiting for transfers between devices, swap_core(): return lax.ppermute(array, BOTH, pairs)  4.08 us
    pallas_call x1, Pallas kernels, per_device(): call(backward_tiles, [((17, T, F), F32), ((17, T, F), F32)], 'ssvv', [plt...  3.21 us
  transfers between devices with their start and end apart: 2, of which 2 were waited for; matrix products, arithmetic and copies ran while one was open for 0% of the time, Pallas kernels for 0%

profile of v1, /device:TPU:1, one launch (start us, length us, event | category | flops | bytes accessed | tf_op | source)
XLA Modules:
  0.0 151.6 jit_solution(17735007014131859008)
XLA Ops:
  0.6 13.2 %all-gather = bf16[512,128]{1,0:T(8,128)(2,1)S(1)} all-gather(bf16[128,128]{1,0:T(8,128)(2,1)} %param.6), channel_id=2, replica_groups={{0,32,64,96},{1,33,65,97},{2,34,66,98},{3,35,67,99},{4,36,68,100},{5,37..., dimensions={0}, use_global_device_ids=true | all-gather | bytes 163840 | tf_op jit(solution)/shard_map/all_gather | solution.py:44
  13.8 10.3 %all-gather.1.own = bf16[16,128,128]{2,1,0:T(8,128)(2,1)S(1)} all-gather(bf16[4,128,128]{2,1,0:T(8,128)(2,1)S(1)} %bitcast.12), channel_id=3, replica_groups={{0,128,256,384},{1,129,257,385},{2,130,258,386},{3,131,259,387},{4,132,..., dimensions={0}, use_global_device_ids=true | all-gather | bytes 655360 | tf_op jit(solution)/shard_map/all_gather | solution.py:44
  24.2 0.0 copy-start
  24.2 11.8 %collective-permute-start = (bf16[16,128,128]{2,1,0:T(8,128)(2,1)S(1)}, bf16[16,128,128]{2,1,0:T(8,128)(2,1)S(1)}, u32[]{:S(2)}, u32[]{:S(2)}) collective-permute-start(bf16[16,128,128]{2,1,0:T(8,128)(2,1)S(1)} %all-gather.1.own), channel_id=1, source_target_pairs={{0,16},{1,17},{2,18},{3,19},{4,20},{5,21},{6,22},{7,23},{8,24},{9,... | collective-permute-start | bytes 1572872 | tf_op jit(solution)/shard_map/ppermute | solution.py:40
  36.0 1.5 collective-permute-done.other
  37.5 0.0 copy-start.2
  37.5 0.0 copy-done
  37.5 0.8 copy-done.2
  38.3 2.6 %shard_map.85 = bf16[16,128,128]{2,1,0:T(8,128)(2,1)} custom-call(s32[16]{0:T(128)} %bitcast.13, s32[16]{0:T(128)} %bitcast.15, bf16[16,128,128]{2,1,0:T(8,128)(2,1)} %bitcast.9, bf16[16,128,128]{2,1,0:T(8,128)(2,1)} %copy-done, bf16[16,128,128]{2,1,0:T(8,128)(2,1)} %copy-done.2), custom_call_target="tpu_custom_call" | custom-call | tf_op jit(solution)/shard_map/pallas_call | solution.py:165
  40.9 13.4 %all_to_all.15.parts = bf16[4,512,128]{2,1,0:T(8,128)(2,1)} all-to-all(bf16[4,512,128]{2,1,0:T(8,128)(2,1)} %bitcast.11), channel_id=1, replica_groups={{0,4,8,12},{1,5,9,13},{2,6,10,14},{3,7,11,15},{16,20,24,28},{17,21,25,2..., dimensions={0} | all-to-all | bytes 1048576 | tf_op jit(solution)/shard_map/all_to_all | solution.py:48
  54.3 1.8 %shard_map.86 = bf16[640,128]{1,0:T(8,128)(2,1)} custom-call(bf16[4,512,128]{2,1,0:T(8,128)(2,1)} %all_to_all.15.parts, bf16[128,128]{1,0:T(8,128)(2,1)} %cot.1), custom_call_target="tpu_custom_call" | custom-call | tf_op jit(solution)/shard_map/pallas_call | solution.py:169
  56.1 28.8 %all-gather.2 = bf16[2560,128]{1,0:T(8,128)(2,1)} all-gather(bf16[640,128]{1,0:T(8,128)(2,1)} %shard_map.86), channel_id=4, replica_groups={{0,1,2,3},{4,5,6,7},{8,9,10,11},{12,13,14,15},{16,17,18,19},{20,21,22,2..., dimensions={0}, use_global_device_ids=true | all-gather | bytes 819200 | tf_op jit(solution)/shard_map/all_gather | solution.py:44
  84.9 2.2 %shard_map.87 = (f32[128,128]{1,0:T(8,128)}, bf16[768,128]{1,0:T(8,128)(2,1)}) custom-call(bf16[4,640,128]{2,1,0:T(8,128)(2,1)} %bitcast.8, bf16[128,128]{1,0:T(8,128)(2,1)} %weight.1), custom_call_target="tpu_custom_call" | custom-call | tf_op jit(solution)/shard_map/pallas_call | solution.py:171
  87.1 11.5 %all-gather.3 = bf16[3072,128]{1,0:T(8,128)(2,1)} all-gather(bf16[768,128]{1,0:T(8,128)(2,1)} %get-tuple-element.10), channel_id=5, replica_groups={{0,4,8,12},{1,5,9,13},{2,6,10,14},{3,7,11,15},{16,20,24,28},{17,21,25,2..., dimensions={0}, use_global_device_ids=true | all-gather | bytes 983040 | tf_op jit(solution)/shard_map/all_gather | solution.py:44
  98.6 3.2 %shard_map.88 = (f32[17,128,128]{2,1,0:T(8,128)}, f32[17,128,128]{2,1,0:T(8,128)}) custom-call(s32[16]{0:T(128)} %bitcast.14, s32[16]{0:T(128)} %bitcast.16, bf16[16,128,128]{2,1,0:T(8,128)(2,1)} %bitcast.10, bf16[4,768,128]{2,1,0:T(8,128)(2,1)} %bitcast.7), custom_call_target="tpu_custom_call" | custom-call | tf_op jit(solution)/shard_map/pallas_call | solution.py:175
  101.8 9.2 %collective-permute-start.1 = (f32[17,128,128]{2,1,0:T(8,128)}, f32[17,128,128]{2,1,0:T(8,128)S(1)}, u32[]{:S(2)}, u32[]{:S(2)}) collective-permute-start(f32[17,128,128]{2,1,0:T(8,128)} %get-tuple-element.12), channel_id=1, source_target_pairs={{0,16},{1,17},{2,18},{3,19},{4,20},{5,21},{6,22},{7,23},{8,24},{9,... | collective-permute-start | bytes 3342344 | tf_op jit(solution)/shard_map/ppermute | solution.py:40
  111.0 2.6 %collective-permute-done.1.got = f32[17,128,128]{2,1,0:T(8,128)S(1)} collective-permute-done((f32[17,128,128]{2,1,0:T(8,128)}, f32[17,128,128]{2,1,0:T(8,128)S(1)}, u32[]{:S(2)}, u32[]{:S(2)}) %collective-permute-start.1) | collective-permute-done | bytes 1114144 | tf_op jit(solution)/shard_map/ppermute | solution.py:40
  113.6 0.0 copy-start.1
  113.6 1.0 copy-done.1
  114.6 2.6 %shard_map.89 = bf16[4,6,128,128]{3,2,1,0:T(8,128)(2,1)} custom-call(f32[17,128,128]{2,1,0:T(8,128)} %get-tuple-element.11.keep, f32[17,128,128]{2,1,0:T(8,128)} %copy-done.1), custom_call_target="tpu_custom_call" | custom-call | tf_op jit(solution)/shard_map/pallas_call | solution.py:182
  117.2 16.3 %all_to_all.16.parts = bf16[4,6,128,128]{3,2,1,0:T(8,128)(2,1)} all-to-all(bf16[4,6,128,128]{3,2,1,0:T(8,128)(2,1)} %shard_map.89), channel_id=1, replica_groups={{0,128,256,384},{1,129,257,385},{2,130,258,386},{3,131,259,387},{4,132,..., dimensions={0} | all-to-all | bytes 1572864 | tf_op jit(solution)/shard_map/all_to_all | solution.py:48
  133.4 2.0 %shard_map.90 = bf16[4,3,128,128]{3,2,1,0:T(8,128)(2,1)} custom-call(bf16[4,6,128,128]{3,2,1,0:T(8,128)(2,1)} %all_to_all.16.parts), custom_call_target="tpu_custom_call" | custom-call | tf_op jit(solution)/shard_map/pallas_call | solution.py:184
  135.4 14.5 %all_to_all.17.parts = bf16[4,3,128,128]{3,2,1,0:T(8,128)(2,1)} all-to-all(bf16[4,3,128,128]{3,2,1,0:T(8,128)(2,1)} %shard_map.90), channel_id=1, replica_groups={{0,32,64,96},{1,33,65,97},{2,34,66,98},{3,35,67,99},{4,36,68,100},{5,37..., dimensions={0} | all-to-all | bytes 786432 | tf_op jit(solution)/shard_map/all_to_all | solution.py:48
  149.9 1.7 %shard_map.91 = (f32[128,128]{1,0:T(8,128)}, f32[128,128]{1,0:T(8,128)}) custom-call(bf16[4,3,128,128]{3,2,1,0:T(8,128)(2,1)} %all_to_all.17.parts), custom_call_target="tpu_custom_call" | custom-call | tf_op jit(solution)/shard_map/pallas_call | solution.py:186
Async XLA Ops:
  24.2 13.4 %copy-start = (bf16[16,128,128]{2,1,0:T(8,128)(2,1)}, bf16[16,128,128]{2,1,0:T(8,128)(2,1)S(1)}, u32[]{:S(2)}) copy-start(bf16[16,128,128]{2,1,0:T(8,128)(2,1)S(1)} %all-gather.1.own) | copy-start | bytes 1572868
  24.2 13.4 %collective-permute-start = (bf16[16,128,128]{2,1,0:T(8,128)(2,1)S(1)}, bf16[16,128,128]{2,1,0:T(8,128)(2,1)S(1)}, u32[]{:S(2)}, u32[]{:S(2)}) collective-permute-start(bf16[16,128,128]{2,1,0:T(8,128)(2,1)S(1)} %all-gather.1.own), channel_id=1, source_target_pairs={{0,16},{1,17},{2,18},{3,19},{4,20},{5,21},{6,22},{7,23},{8,24},{9,... | collective-permute-start | bytes 1572872 | tf_op jit(solution)/shard_map/ppermute | solution.py:40
  37.5 0.8 copy-start.2
  101.8 11.8 %collective-permute-start.1 = (f32[17,128,128]{2,1,0:T(8,128)}, f32[17,128,128]{2,1,0:T(8,128)S(1)}, u32[]{:S(2)}, u32[]{:S(2)}) collective-permute-start(f32[17,128,128]{2,1,0:T(8,128)} %get-tuple-element.12), channel_id=1, source_target_pairs={{0,16},{1,17},{2,18},{3,19},{4,20},{5,21},{6,22},{7,23},{8,24},{9,... | collective-permute-start | bytes 3342344 | tf_op jit(solution)/shard_map/ppermute | solution.py:40
  113.6 1.0 copy-start.1

commit v2 on v1

v2 whole, which is shorter than its diff:
```python
import itertools

import jax
import jax.numpy as jnp
from jax import lax
from jax.experimental import pallas as pl
from jax.experimental.pallas import tpu as pltpu
from jax.sharding import PartitionSpec as P

BOTH = ("row", "col")
SIZES = {"x": 4, "zl": 4, "core": 2, "y": 4, "zh": 4}
F = 128
T = 128
BF = jnp.bfloat16
F32 = jnp.float32


def position(place):
    n = 0
    for name, size in SIZES.items():
        n = n * size + place[name]
    return n


def places():
    for values in itertools.product(*(range(s) for s in SIZES.values())):
        yield dict(zip(SIZES, values))


def groups(axis):
    found = {}
    for place in places():
        key = tuple(v for n, v in place.items() if n != axis)
        found.setdefault(key, []).append(position(place))
    return list(found.values())


def swap_core(array):
    pairs = [(position(p), position({**p, "core": 1 - p["core"]})) for p in places()]
    return lax.ppermute(array, BOTH, pairs)


def gather(array, axis):
    return exchange(jnp.broadcast_to(array[None], (4, *array.shape)), axis)


def exchange(array, axis):
    return lax.all_to_all(array, BOTH, 0, 0, tiled=True, axis_index_groups=groups(axis))


def dot(a, b, dims):
    return lax.dot_general(a, b, (dims, ((), ())), preferred_element_type=F32)


def call(body, outs, spaces, scratch=()):
    kinds = {"v": pltpu.VMEM, "s": pltpu.SMEM}
    return pl.pallas_call(
        body,
        out_shape=[jax.ShapeDtypeStruct(s, d) for s, d in outs],
        in_specs=[pl.BlockSpec(memory_space=kinds[k]) for k in spaces],
        out_specs=[pl.BlockSpec(memory_space=pltpu.VMEM) for _ in outs],
        scratch_shapes=list(scratch),
    )


def forward_tiles(rows, cols, adj, own, other, out, mine, acc):
    core = lax.rem(lax.axis_index("row"), 2)
    acc[...] = jnp.zeros_like(acc)
    for t in range(16):
        b = cols[t]
        spot = lax.div(b, 2)
        x = jnp.where(lax.rem(b, 2) == core, own[spot], other[spot])
        r = rows[t]
        acc[r] += dot(adj[t], x, ((1,), (0,)))
    out[...] = acc[...].astype(BF).reshape(4, 4, T, F)
    mine[...] = acc[pl.ds(lax.div(lax.axis_index("col"), 4) * 4, 4)]


def layer(parts, cots, weight, act, out, kept):
    total = parts[0].astype(F32)
    for k in range(1, 4):
        total += parts[k].astype(F32)
    zed = total.reshape(512, F).astype(BF)
    w = weight[...]
    pre = dot(zed, w, ((1,), (0,)))
    sig = jax.nn.sigmoid(pre)
    kept[...] = (pre * sig).reshape(4, T, F)
    act[...] = kept[lax.rem(lax.axis_index("col"), 4)]
    cot = cots[...].reshape(512, F)
    dpre = (cot.astype(F32) * sig * (1.0 + pre * (1.0 - sig))).astype(BF)
    back = dot(dpre, w, ((1,), (1,))).astype(BF).reshape(4, T, F)
    grad = dot(zed, dpre, ((0,), (0,)))
    high, low = split(grad)
    for k in range(4):
        out[k, pl.ds(0, 4)] = back
        out[k, 4] = high
        out[k, 5] = low


def backward_tiles(rows, cols, adj, parts, keep, send, acc):
    core = lax.rem(lax.axis_index("row"), 2)
    acc[...] = jnp.zeros_like(acc)
    for t in range(16):
        r = rows[t]
        b = cols[t]
        d = parts[lax.div(r, 4), lax.rem(r, 4)]
        acc[lax.rem(b, 2), lax.div(b, 2)] += dot(adj[t], d, ((0,), (0,)))
    keep[pl.ds(0, 16)] = acc[core]
    send[pl.ds(0, 16)] = acc[1 - core]
    grad = jnp.zeros((F, F), F32)
    for k in range(4):
        grad += parts[k, 4].astype(F32) + parts[k, 5].astype(F32)
    keep[16] = grad
    send[16] = grad


def split(grad):
    high = grad.astype(BF)
    return high, (grad - high.astype(F32)).astype(BF)


def spread(array):
    return jnp.broadcast_to(array[None], (4, *array.shape))


def add_received(own, parts, place):
    others = jnp.arange(4).reshape(4, 1, 1, 1) != place
    return own + jnp.sum(jnp.where(others, parts.astype(F32), 0.0), axis=0)


def per_device(features, weight, adj_values, tile_rows, tile_cols, cotangent):
    adj = adj_values.reshape(16, T, T)
    rows = tile_rows.reshape(16)
    cols = tile_cols.reshape(16)
    x_place = lax.axis_index("row") // 8
    y_place = lax.axis_index("col") // 4

    own = gather(gather(features, "zl"), "x").reshape(16, T, F)
    other = swap_core(own)
    partial, mine = call(
        forward_tiles,
        [((4, 4, T, F), BF), ((4, T, F), F32)],
        "ssvvv",
        [pltpu.VMEM((16, T, F), F32)],
    )(rows, cols, adj, own, other)
    parts = exchange(partial, "y")
    summed = add_received(mine, parts, y_place).astype(BF)
    parts = gather(jnp.concatenate([summed, cotangent[None]], axis=0), "zh")
    act, back = call(
        layer,
        [((T, F), F32), ((4, 6, T, F), BF)],
        "vvv",
        [pltpu.VMEM((4, T, F), F32)],
    )(parts[:, :4], parts[:, 4], weight)
    parts = exchange(back, "y")
    keep, send = call(
        backward_tiles,
        [((17, T, F), F32), ((17, T, F), F32)],
        "ssvv",
        [pltpu.VMEM((2, 16, T, F), F32)],
    )(rows, cols, adj, parts)
    total = keep + swap_core(send)
    tiles = total[:16].reshape(4, 4, T, F)
    high, low = split(total[16])
    parts = exchange(
        jnp.concatenate([tiles.astype(BF), spread(jnp.stack([high, low]))], axis=1), "x"
    )
    mine = lax.dynamic_index_in_dim(tiles, x_place, 0, keepdims=False)
    tiles = add_received(mine, parts[:, :4], x_place).astype(BF)
    high, low = split(jnp.sum(parts[:, 4:].astype(F32), axis=(0, 1)))
    parts = exchange(
        jnp.concatenate([tiles[:, None], spread(jnp.stack([high, low]))], axis=1), "zl"
    )
    parts = parts.astype(F32)
    out = jnp.sum(parts[:, 0], axis=0)
    grad = jnp.sum(parts[:, 1:], axis=(0, 1))
    return act, out, grad


def solution(mesh):
    return jax.shard_map(
        per_device,
        mesh=mesh,
        in_specs=(
            P(BOTH, None),
            P(),
            P("row", "col", None, None, None),
            P("row", "col", None),
            P("row", "col", None),
            P(BOTH, None),
        ),
        out_specs=(P(BOTH, None), P(BOTH, None), P()),
        check_vma=False,
    )
```

time: 152 us -> 160 us (1.053)
  waiting for transfers between devices: 4.08 us -> 25 us
  blocking collectives: 108 us -> 99.7 us
  Pallas kernels: 16 us -> 8.35 us
  other arithmetic: 0 us -> 4.4 us
  starting transfers between devices: 21 us -> 17.2 us
  local copies, waits for them, and re-layouts: 1.83 us -> 3.45 us
    all_gather x4 -> x0, blocking collectives: 63.9 us -> none  [gather(): lax.all_gather(array, BOTH, axis=0, tiled=False, axis_index_groups=groups...]
    all_to_all x3 -> x5, blocking collectives: 44.2 us -> 99.7 us  [exchange(): lax.all_to_all(array, BOTH, 0, 0, tiled=True, axis_index_groups=groups(ax...]
    all_to_all x0 -> x2, waiting for transfers between devices: none -> 20.9 us  [exchange(): lax.all_to_all(array, BOTH, 0, 0, tiled=True, axis_index_groups=groups(ax...]
    ppermute x2, starting transfers between devices: 21 us -> 9.62 us  [swap_core(): return lax.ppermute(array, BOTH, pairs)]
    pallas_call x6 -> x2, Pallas kernels: 12.8 us -> 5.13 us  [the longest x1 2.73 us: per_device(): call(forward_tiles, [((4, 4, T, F), BF), ((4, T, F), F32)], 'ssvvv', [plt...]
    all_to_all x0 -> x2, starting transfers between devices: none -> 7.62 us  [exchange(): lax.all_to_all(array, BOTH, 0, 0, tiled=True, axis_index_groups=groups(ax...]
    reduce_sum x0 -> x5, other arithmetic: none -> 1.7 us  [the longest x1 0.66 us: per_device(): grad = jnp.sum(parts[:, 1:], axis=(0, 1))]
  transfers between devices with their start and end apart: 2 -> 4, of which waited for: 2 -> 4; matrix products, arithmetic and copies ran while one was open for 0% -> 0% of each run, Pallas kernels for 0% -> 0%
where the time goes in v2:
time: 160 us; the launch traced here: 159 us
  blocking collectives  99.7 us (62%)
  waiting for transfers between devices  25 us (16%)
  starting transfers between devices  17.2 us (11%)
  Pallas kernels  8.35 us (5%)
  other arithmetic  4.4 us (3%)
  local copies, waits for them, and re-layouts  3.45 us (2%)
    all_to_all x5, blocking collectives, exchange(): lax.all_to_all(array, BOTH, 0, 0, tiled=True, axis_index_groups=groups(ax...  99.7 us
    all_to_all x2, waiting for transfers between devices, exchange(): lax.all_to_all(array, BOTH, 0, 0, tiled=True, axis_index_groups=groups(ax...  20.9 us
    ppermute x2, starting transfers between devices, swap_core(): return lax.ppermute(array, BOTH, pairs)  9.62 us
    all_to_all x2, starting transfers between devices, exchange(): lax.all_to_all(array, BOTH, 0, 0, tiled=True, axis_index_groups=groups(ax...  7.62 us
    ppermute x2, waiting for transfers between devices, swap_core(): return lax.ppermute(array, BOTH, pairs)  4.08 us
    pallas_call x1, Pallas kernels, per_device(): call(backward_tiles, [((17, T, F), F32), ((17, T, F), F32)], 'ssvv', [plt...  3.23 us
  transfers between devices with their start and end apart: 4, of which 4 were waited for; matrix products, arithmetic and copies ran while one was open for 0% of the time, Pallas kernels for 0%

profile of v2, /device:TPU:1, one launch (start us, length us, event | category | flops | bytes accessed | tf_op | source)
XLA Modules:
  0.0 158.9 jit_solution(12827980741194445916)
XLA Ops:
  0.6 0.8 broadcast_in_dim.52
  1.4 11.0 %all_to_all.35 = bf16[4,128,128]{2,1,0:T(8,128)(2,1)S(1)} all-to-all(bf16[4,128,128]{2,1,0:T(8,128)(2,1)S(1)} %broadcast_in_dim.52), channel_id=1, replica_groups={{0,32,64,96},{1,33,65,97},{2,34,66,98},{3,35,67,99},{4,36,68,100},{5,37..., dimensions={0} | all-to-all | bytes 262144 | tf_op jit(solution)/shard_map/all_to_all | solution.py:48
  12.4 0.1 broadcast_in_dim.53
  12.5 10.7 %all_to_all.36 = bf16[4,4,128,128]{3,2,1,0:T(8,128)(2,1)S(1)} all-to-all(bf16[4,4,128,128]{3,2,1,0:T(8,128)(2,1)S(1)} %broadcast_in_dim.53), channel_id=1, replica_groups={{0,128,256,384},{1,129,257,385},{2,130,258,386},{3,131,259,387},{4,132,..., dimensions={0} | all-to-all | bytes 1048576 | tf_op jit(solution)/shard_map/all_to_all | solution.py:48
  23.3 0.0 copy-start
  23.3 5.8 %collective-permute-start = (bf16[16,128,128]{2,1,0:T(8,128)(2,1)S(1)}, bf16[16,128,128]{2,1,0:T(8,128)(2,1)S(1)}, u32[]{:S(2)}, u32[]{:S(2)}) collective-permute-start(bf16[16,128,128]{2,1,0:T(8,128)(2,1)S(1)} %bitcast.26), channel_id=1, source_target_pairs={{0,16},{1,17},{2,18},{3,19},{4,20},{5,21},{6,22},{7,23},{8,24},{9,... | collective-permute-start | bytes 1572872 | tf_op jit(solution)/shard_map/ppermute | solution.py:40
  29.0 1.5 collective-permute-done.other
  30.6 0.0 copy-start.1
  30.6 0.0 copy-done
  30.6 0.8 copy-done.1
  31.4 2.7 %shard_map.85 = (bf16[4,4,128,128]{3,2,1,0:T(8,128)(2,1)}, f32[4,128,128]{2,1,0:T(8,128)}) custom-call(s32[16]{0:T(128)} %bitcast.29, s32[16]{0:T(128)} %bitcast.31, bf16[16,128,128]{2,1,0:T(8,128)(2,1)} %bitcast.24, bf16[16,128,128]{2,1,0:T(8,128)(2,1)} %bitcast.27, bf16[16,128,128]{2,1,0:T(8,128)(2,1)} %copy-done.1), custom_call_target="tpu_custom_call" | custom-call | tf_op jit(solution)/shard_map/pallas_call | solution.py:140
  34.1 0.0 copy-start.2
  34.1 0.0 copy-start.3
  34.1 4.1 %all-to-all-start.2 = ((bf16[4,4,128,128]{3,2,1,0:T(8,128)(2,1)}), bf16[4,4,128,128]{3,2,1,0:T(8,128)(2,1)S(1)}, u32[]{:S(2)}, u32[]{:S(2)}) async-start(bf16[4,4,128,128]{3,2,1,0:T(8,128)(2,1)} %get-tuple-element.10), calls=%async_computation.2 | async-start | bytes 1048576 | tf_op jit(solution)/shard_map/all_to_all | solution.py:48
  38.2 8.9 %all-to-all-done.2 = bf16[4,4,128,128]{3,2,1,0:T(8,128)(2,1)S(1)} async-done(((bf16[4,4,128,128]{3,2,1,0:T(8,128)(2,1)}), bf16[4,4,128,128]{3,2,1,0:T(8,128)(2,1)S(1)}, u32[]{:S(2)}, u32[]{:S(2)}) %all-to-all-start.2) | async-done | bytes 524320 | tf_op jit(solution)/shard_map/all_to_all | solution.py:48
  47.2 0.2 select_reduce_fusion.1
  47.3 0.0 copy-done.2
  47.4 0.0 copy-done.3
  47.4 0.1 broadcast_in_dim.57
  47.6 44.2 %all_to_all.37 = bf16[4,5,128,128]{3,2,1,0:T(8,128)(2,1)S(1)} all-to-all(bf16[4,5,128,128]{3,2,1,0:T(8,128)(2,1)S(1)} %broadcast_in_dim.57), channel_id=1, replica_groups={{0,1,2,3},{4,5,6,7},{8,9,10,11},{12,13,14,15},{16,17,18,19},{20,21,22,2..., dimensions={0} | all-to-all | bytes 1310720 | tf_op jit(solution)/shard_map/all_to_all | solution.py:48
  91.7 0.8 slice.32.parts
  92.6 0.7 slice_bitcast_fusion.cots
  93.2 2.4 %shard_map.86 = (f32[128,128]{1,0:T(8,128)}, bf16[4,6,128,128]{3,2,1,0:T(8,128)(2,1)}) custom-call(bf16[4,4,128,128]{3,2,1,0:T(8,128)(2,1)} %slice.32.parts, bf16[4,128,128]{2,1,0:T(8,128)(2,1)} %slice_bitcast_fusion.cots, bf16[128,128]{1,0:T(8,128)(2,1)} %weight.1), custom_call_target="tpu_custom_call" | custom-call | tf_op jit(solution)/shard_map/pallas_call | solution.py:149
  95.6 15.5 %all_to_all.38.parts = bf16[4,6,128,128]{3,2,1,0:T(8,128)(2,1)} all-to-all(bf16[4,6,128,128]{3,2,1,0:T(8,128)(2,1)} %get-tuple-element.12), channel_id=1, replica_groups={{0,4,8,12},{1,5,9,13},{2,6,10,14},{3,7,11,15},{16,20,24,28},{17,21,25,2..., dimensions={0} | all-to-all | bytes 1572864 | tf_op jit(solution)/shard_map/all_to_all | solution.py:48
  111.2 3.2 %shard_map.87 = (f32[17,128,128]{2,1,0:T(8,128)}, f32[17,128,128]{2,1,0:T(8,128)}) custom-call(s32[16]{0:T(128)} %bitcast.30, s32[16]{0:T(128)} %bitcast.32, bf16[16,128,128]{2,1,0:T(8,128)(2,1)} %bitcast.25, bf16[4,6,128,128]{3,2,1,0:T(8,128)(2,1)} %all_to_all.38.parts), custom_call_target="tpu_custom_call" | custom-call | tf_op jit(solution)/shard_map/pallas_call | solution.py:156
  114.4 3.8 %collective-permute-start.1 = (f32[17,128,128]{2,1,0:T(8,128)}, f32[17,128,128]{2,1,0:T(8,128)S(1)}, u32[]{:S(2)}, u32[]{:S(2)}) collective-permute-start(f32[17,128,128]{2,1,0:T(8,128)} %get-tuple-element.14), channel_id=1, source_target_pairs={{0,16},{1,17},{2,18},{3,19},{4,20},{5,21},{6,22},{7,23},{8,24},{9,... | collective-permute-start | bytes 3342344 | tf_op jit(solution)/shard_map/ppermute | solution.py:40
  118.2 2.6 %collective-permute-done.1 = f32[17,128,128]{2,1,0:T(8,128)S(1)} collective-permute-done((f32[17,128,128]{2,1,0:T(8,128)}, f32[17,128,128]{2,1,0:T(8,128)S(1)}, u32[]{:S(2)}, u32[]{:S(2)}) %collective-permute-start.1) | collective-permute-done | bytes 1114144 | tf_op jit(solution)/shard_map/ppermute | solution.py:40
  120.8 1.4 add.23
  122.2 0.1 slice.34
  122.3 0.1 convert_element_type.77
  122.5 1.0 pad_maximum_fusion
  123.4 3.5 %all-to-all-start.5 = ((bf16[4,6,128,128]{3,2,1,0:T(8,128)(2,1)}), bf16[4,6,128,128]{3,2,1,0:T(8,128)(2,1)S(1)}, u32[]{:S(2)}, u32[]{:S(2)}) async-start(bf16[4,6,128,128]{3,2,1,0:T(8,128)(2,1)} %pad_maximum_fusion), calls=%async_computation.5 | async-start | bytes 1572864 | tf_op jit(solution)/shard_map/all_to_all | solution.py:48
  127.0 11.9 %all-to-all-done.5 = bf16[4,6,128,128]{3,2,1,0:T(8,128)(2,1)S(1)} async-done(((bf16[4,6,128,128]{3,2,1,0:T(8,128)(2,1)}), bf16[4,6,128,128]{3,2,1,0:T(8,128)(2,1)S(1)}, u32[]{:S(2)}, u32[]{:S(2)}) %all-to-all-start.5) | async-done | bytes 786464 | tf_op jit(solution)/shard_map/all_to_all | solution.py:48
  139.0 0.2 select_reduce_fusion
  139.3 18.2 %all_to_all.39 = bf16[4,3,128,128]{3,2,1,0:T(8,128)(2,1)S(1)} all-to-all(bf16[4,3,128,128]{3,2,1,0:T(8,128)(2,1)S(1)} %pad_maximum_fusion.1), channel_id=1, replica_groups={{0,32,64,96},{1,33,65,97},{2,34,66,98},{3,35,67,99},{4,36,68,100},{5,37..., dimensions={0} | all-to-all | bytes 786432 | tf_op jit(solution)/shard_map/all_to_all | solution.py:48
  157.5 0.1 convert_element_type.87
  157.6 0.6 slice_reduce_fusion.1
  158.3 0.7 slice_reduce_fusion
  (13 shorter events, 0.3 us)
Async XLA Ops:
  23.3 7.3 %copy-start = (bf16[4,4,128,128]{3,2,1,0:T(8,128)(2,1)}, bf16[4,4,128,128]{3,2,1,0:T(8,128)(2,1)S(1)}, u32[]{:S(2)}) copy-start(bf16[4,4,128,128]{3,2,1,0:T(8,128)(2,1)S(1)} %all_to_all.36) | copy-start | bytes 1572868
  23.3 7.3 %collective-permute-start = (bf16[16,128,128]{2,1,0:T(8,128)(2,1)S(1)}, bf16[16,128,128]{2,1,0:T(8,128)(2,1)S(1)}, u32[]{:S(2)}, u32[]{:S(2)}) collective-permute-start(bf16[16,128,128]{2,1,0:T(8,128)(2,1)S(1)} %bitcast.26), channel_id=1, source_target_pairs={{0,16},{1,17},{2,18},{3,19},{4,20},{5,21},{6,22},{7,23},{8,24},{9,... | collective-permute-start | bytes 1572872 | tf_op jit(solution)/shard_map/ppermute | solution.py:40
  30.6 0.8 copy-start.1
  34.1 13.3 %copy-start.2 = (f32[4,128,128]{2,1,0:T(8,128)S(1)}, f32[4,128,128]{2,1,0:T(8,128)}, u32[]{:S(2)}) copy-start(f32[4,128,128]{2,1,0:T(8,128)} %get-tuple-element.9) | copy-start | bytes 786436
  34.1 13.3 %copy-start.3 = (bf16[128,128]{1,0:T(8,128)(2,1)S(1)}, bf16[128,128]{1,0:T(8,128)(2,1)}, u32[]{:S(2)}) copy-start(bf16[128,128]{1,0:T(8,128)(2,1)} %param.11) | copy-start | bytes 98308
  34.1 13.1 %all-to-all-start.2 = ((bf16[4,4,128,128]{3,2,1,0:T(8,128)(2,1)}), bf16[4,4,128,128]{3,2,1,0:T(8,128)(2,1)S(1)}, u32[]{:S(2)}, u32[]{:S(2)}) async-start(bf16[4,4,128,128]{3,2,1,0:T(8,128)(2,1)} %get-tuple-element.10), calls=%async_computation.2 | async-start | bytes 1048576 | tf_op jit(solution)/shard_map/all_to_all | solution.py:48
  114.4 6.4 %collective-permute-start.1 = (f32[17,128,128]{2,1,0:T(8,128)}, f32[17,128,128]{2,1,0:T(8,128)S(1)}, u32[]{:S(2)}, u32[]{:S(2)}) collective-permute-start(f32[17,128,128]{2,1,0:T(8,128)} %get-tuple-element.14), channel_id=1, source_target_pairs={{0,16},{1,17},{2,18},{3,19},{4,20},{5,21},{6,22},{7,23},{8,24},{9,... | collective-permute-start | bytes 3342344 | tf_op jit(solution)/shard_map/ppermute | solution.py:40
  123.4 15.5 %all-to-all-start.5 = ((bf16[4,6,128,128]{3,2,1,0:T(8,128)(2,1)}), bf16[4,6,128,128]{3,2,1,0:T(8,128)(2,1)S(1)}, u32[]{:S(2)}, u32[]{:S(2)}) async-start(bf16[4,6,128,128]{3,2,1,0:T(8,128)(2,1)} %pad_maximum_fusion), calls=%async_computation.5 | async-start | bytes 1572864 | tf_op jit(solution)/shard_map/all_to_all | solution.py:48

commit v3 on v2

v3 whole, which is shorter than its diff:
```python
import itertools

import jax
import jax.numpy as jnp
from jax import lax
from jax.experimental import pallas as pl
from jax.experimental.pallas import tpu as pltpu
from jax.sharding import PartitionSpec as P

BOTH = ("row", "col")
SIZES = {"x": 4, "zl": 4, "core": 2, "y": 4, "zh": 4}
F = 128
T = 128
BF = jnp.bfloat16
F32 = jnp.float32


def position(place):
    n = 0
    for name, size in SIZES.items():
        n = n * size + place[name]
    return n


def places():
    for values in itertools.product(*(range(s) for s in SIZES.values())):
        yield dict(zip(SIZES, values))


def groups(axis):
    found = {}
    for place in places():
        key = tuple(v for n, v in place.items() if n != axis)
        found.setdefault(key, []).append(position(place))
    return list(found.values())


def swap_core(array):
    pairs = [(position(p), position({**p, "core": 1 - p["core"]})) for p in places()]
    return lax.ppermute(array, BOTH, pairs)


def gather(array, axis):
    return lax.all_gather(array, BOTH, axis=0, tiled=False, axis_index_groups=groups(axis))


def exchange(array, axis):
    return lax.all_to_all(array, BOTH, 0, 0, tiled=True, axis_index_groups=groups(axis))


def spread(array):
    return jnp.broadcast_to(array[None], (4, *array.shape))


def core_place():
    return lax.rem(lax.axis_index("row"), 2)


def zl_place():
    return lax.rem(lax.div(lax.axis_index("row"), 2), 4)


def x_place():
    return lax.div(lax.axis_index("row"), 8)


def zh_place():
    return lax.rem(lax.axis_index("col"), 4)


def y_place():
    return lax.div(lax.axis_index("col"), 4)


def dot(a, b, dims):
    return lax.dot_general(a, b, (dims, ((), ())), preferred_element_type=F32)


def call(body, outs, spaces, scratch=()):
    kinds = {"v": pltpu.VMEM, "s": pltpu.SMEM}
    return pl.pallas_call(
        body,
        out_shape=[jax.ShapeDtypeStruct(s, d) for s, d in outs],
        in_specs=[pl.BlockSpec(memory_space=kinds[k]) for k in spaces],
        out_specs=[pl.BlockSpec(memory_space=pltpu.VMEM) for _ in outs],
        scratch_shapes=list(scratch),
        compiler_params=pltpu.CompilerParams(vmem_limit_bytes=16 << 20),
    )


def split(grad):
    high = grad.astype(BF)
    return high, (grad - high.astype(F32)).astype(BF)


def plus_others(own, parts, place, count):
    for j in range(1, 4):
        own += parts[lax.rem(place + j, 4), pl.ds(0, count)].astype(F32)
    return own


def forward_tiles(rows, cols, adj, own, other, out, mine, acc):
    acc[...] = jnp.zeros_like(acc)
    for t in range(16):
        b = cols[t]
        spot = lax.div(b, 2)
        x = jnp.where(lax.rem(b, 2) == core_place(), own[spot], other[spot])
        r = rows[t]
        acc[r] += dot(adj[t], x, ((1,), (0,)))
    out[...] = acc[...].astype(BF).reshape(4, 4, T, F)
    mine[...] = acc[pl.ds(y_place() * 4, 4)]


def add_y(parts, mine, cot, out):
    out[pl.ds(0, 4)] = plus_others(mine[...], parts, y_place(), 4).astype(BF)
    out[4] = cot[...]


def layer(parts, weight, act, out, kept):
    total = parts[0, pl.ds(0, 4)].astype(F32)
    for k in range(1, 4):
        total += parts[k, pl.ds(0, 4)].astype(F32)
    zed = total.reshape(512, F).astype(BF)
    w = weight[...]
    pre = dot(zed, w, ((1,), (0,)))
    sig = jax.nn.sigmoid(pre)
    kept[...] = (pre * sig).reshape(4, T, F)
    act[...] = kept[zh_place()]
    cot = jnp.concatenate([parts[k, 4] for k in range(4)], axis=0)
    dpre = (cot.astype(F32) * sig * (1.0 + pre * (1.0 - sig))).astype(BF)
    back = dot(dpre, w, ((1,), (1,))).astype(BF).reshape(4, T, F)
    grad = dot(zed, dpre, ((0,), (0,))).astype(BF)
    for k in range(4):
        out[k, pl.ds(0, 4)] = back
        out[k, 4] = grad


def backward_tiles(rows, cols, adj, parts, keep, send, acc, total):
    core = core_place()
    acc[...] = jnp.zeros_like(acc)
    for t in range(16):
        r = rows[t]
        b = cols[t]
        d = parts[lax.div(r, 4), lax.rem(r, 4)]
        acc[lax.rem(b, 2), lax.div(b, 2)] += dot(adj[t], d, ((0,), (0,)))
    grad = parts[0, 4].astype(F32)
    for k in range(1, 4):
        grad += parts[k, 4].astype(F32)
    total[...] = grad.reshape(2, 64, F)
    for ref, c in ((keep, core), (send, 1 - core)):
        ref[pl.ds(0, 2048), :] = acc[c].reshape(2048, F)
        ref[pl.ds(2048, 64), :] = total[c]


def add_cores(keep, got, out, mine):
    total = (keep[pl.ds(0, 2048), :] + got[pl.ds(0, 2048), :]).reshape(4, 4, T, F)
    high, low = split(keep[pl.ds(2048, 64), :] + got[pl.ds(2048, 64), :])
    for k in range(4):
        out[k, pl.ds(0, 4)] = total[k].astype(BF)
        out[k, 4, pl.ds(0, 64), :] = high
        out[k, 4, pl.ds(64, 64), :] = low
    start = pl.multiple_of(x_place() * 512, 512)
    own = keep[pl.ds(start, 512), :] + got[pl.ds(start, 512), :]
    mine[...] = own.reshape(4, T, F)


def sum_halves(parts, spot):
    total = parts[0, spot].astype(F32)
    for k in range(1, 4):
        total += parts[k, spot].astype(F32)
    return total[:64] + total[64:]


def add_x(parts, mine, out, own, kept):
    total = plus_others(mine[...], parts, x_place(), 4)
    high, low = split(sum_halves(parts, 4))
    for k in range(4):
        out[k, 0] = total[k].astype(BF)
        out[k, 1, pl.ds(0, 64), :] = high
        out[k, 1, pl.ds(64, 64), :] = low
    kept[...] = total
    own[...] = kept[zl_place()]


def add_z(parts, own, out, half):
    total = own[...]
    for j in range(1, 4):
        total += parts[lax.rem(zl_place() + j, 4), 0].astype(F32)
    out[...] = total
    half[...] = sum_halves(parts, 1)


def join(half, got, grad):
    core = core_place()
    grad[core] = half[...]
    grad[1 - core] = got[...]


def per_device(features, weight, adj_values, tile_rows, tile_cols, cotangent):
    adj = adj_values.reshape(16, T, T)
    rows = tile_rows.reshape(16)
    cols = tile_cols.reshape(16)
    tile = (T, F)

    own = exchange(spread(exchange(spread(features), "zl")), "x").reshape(16, T, F)
    other = swap_core(own)
    partial, mine = call(
        forward_tiles,
        [((4, 4, T, F), BF), ((4, T, F), F32)],
        "ssvvv",
        [pltpu.VMEM((16, T, F), F32)],
    )(rows, cols, adj, own, other)
    parts = exchange(partial, "y")
    (summed,) = call(add_y, [((5, T, F), BF)], "vvv")(parts, mine, cotangent)
    parts = gather(summed, "zh")
    act, back = call(
        layer, [(tile, F32), ((4, 5, T, F), BF)], "vv", [pltpu.VMEM((4, T, F), F32)]
    )(parts, weight)
    parts = exchange(back, "y")
    keep, send = call(
        backward_tiles,
        [((2112, F), F32), ((2112, F), F32)],
        "ssvv",
        [pltpu.VMEM((2, 16, T, F), F32), pltpu.VMEM((2, 64, F), F32)],
    )(rows, cols, adj, parts)
    got = swap_core(send)
    parts, mine = call(add_cores, [((4, 5, T, F), BF), ((4, T, F), F32)], "vv")(keep, got)
    parts = exchange(parts, "x")
    parts, own = call(
        add_x, [((4, 2, T, F), BF), (tile, F32)], "vv", [pltpu.VMEM((4, T, F), F32)]
    )(parts, mine)
    parts = exchange(parts, "zl")
    out, half = call(add_z, [(tile, F32), ((64, F), F32)], "vv")(parts, own)
    (grad,) = call(join, [((2, 64, F), F32)], "vv")(half, swap_core(half))
    return act, out, grad.reshape(F, F)


def solution(mesh):
    return jax.shard_map(
        per_device,
        mesh=mesh,
        in_specs=(
            P(BOTH, None),
            P(),
            P("row", "col", None, None, None),
            P("row", "col", None),
            P("row", "col", None),
            P(BOTH, None),
        ),
        out_specs=(P(BOTH, None), P(BOTH, None), P()),
        check_vma=False,
    )
```

time: 160 us -> 130 us (0.81)
  waiting for transfers between devices: 25 us -> 4.66 us
  other arithmetic: 4.4 us -> 0 us
  Pallas kernels: 8.35 us -> 4.72 us
  starting transfers between devices: 17.2 us -> 20.4 us
  local copies, waits for them, and re-layouts: 3.45 us -> 0.95 us
  blocking collectives: 99.7 us -> 97.5 us
    all_to_all x5 -> x6, blocking collectives: 99.7 us -> 67.2 us  [exchange(): lax.all_to_all(array, BOTH, 0, 0, tiled=True, axis_index_groups=groups(ax...]
    all_gather x0 -> x1, blocking collectives: none -> 30.3 us  [gather(): lax.all_gather(array, BOTH, axis=0, tiled=False, axis_index_groups=groups...]
    all_to_all x2 -> x0, waiting for transfers between devices: 20.9 us -> none  [exchange(): lax.all_to_all(array, BOTH, 0, 0, tiled=True, axis_index_groups=groups(ax...]
    ppermute x2 -> x3, starting transfers between devices: 9.62 us -> 20.4 us  [swap_core(): return lax.ppermute(array, BOTH, pairs)]
    all_to_all x2 -> x0, starting transfers between devices: 7.62 us -> none  [exchange(): lax.all_to_all(array, BOTH, 0, 0, tiled=True, axis_index_groups=groups(ax...]
    pallas_call x2 -> x7, Pallas kernels: 5.62 us -> 3.72 us  [the longest x1 1.14 us: per_device(): call(backward_tiles, [((2112, F), F32), ((2112, F), F32)], 'ssvv', [pltpu...]
    pallas_call x1, Pallas kernels: 2.73 us -> 1 us  [per_device(): call(forward_tiles, [((4, 4, T, F), BF), ((4, T, F), F32)], 'ssvvv', [plt...]
    reduce_sum x5 -> x0, other arithmetic: 1.7 us -> none  [the longest x1 0.66 us: per_device(): grad = jnp.sum(parts[:, 1:], axis=(0, 1))]
  transfers between devices with their start and end apart: 4 -> 3, of which waited for: 4 -> 3; matrix products, arithmetic and copies ran while one was open for 0% -> 0% of each run, Pallas kernels for 0% -> 0%
where the time goes in v3:
time: 130 us; the launch traced here: 129 us
  blocking collectives  97.5 us (75%)
  starting transfers between devices  20.4 us (16%)
  Pallas kernels  4.72 us (4%)
  waiting for transfers between devices  4.66 us (4%)
    all_to_all x6, blocking collectives, exchange(): lax.all_to_all(array, BOTH, 0, 0, tiled=True, axis_index_groups=groups(ax...  67.2 us
    all_gather x1, blocking collectives, gather(): lax.all_gather(array, BOTH, axis=0, tiled=False, axis_index_groups=groups...  30.3 us
    ppermute x3, starting transfers between devices, swap_core(): return lax.ppermute(array, BOTH, pairs)  20.4 us
    ppermute x3, waiting for transfers between devices, swap_core(): return lax.ppermute(array, BOTH, pairs)  4.66 us
  transfers between devices with their start and end apart: 3, of which 3 were waited for; matrix products, arithmetic and copies ran while one was open for 0% of the time, Pallas kernels for 0%

profile of v3, /device:TPU:1, one launch (start us, length us, event | category | flops | bytes accessed | tf_op | source)
XLA Modules:
  0.0 129.0 jit_solution(13338762839167001330)
XLA Ops:
  0.6 0.0 copy-start.4
  0.6 0.0 copy-start.3
  0.7 0.0 copy-start
  0.7 0.8 broadcast_in_dim.4
  1.5 11.0 %all_to_all.30 = bf16[4,128,128]{2,1,0:T(8,128)(2,1)S(1)} all-to-all(bf16[4,128,128]{2,1,0:T(8,128)(2,1)S(1)} %broadcast_in_dim.4), channel_id=1, replica_groups={{0,32,64,96},{1,33,65,97},{2,34,66,98},{3,35,67,99},{4,36,68,100},{5,37..., dimensions={0} | all-to-all | bytes 262144 | tf_op jit(solution)/shard_map/all_to_all | solution.py:48
  12.5 0.1 broadcast_in_dim.5
  12.6 10.7 %all_to_all.31 = bf16[4,4,128,128]{3,2,1,0:T(8,128)(2,1)S(1)} all-to-all(bf16[4,4,128,128]{3,2,1,0:T(8,128)(2,1)S(1)} %broadcast_in_dim.5), channel_id=1, replica_groups={{0,128,256,384},{1,129,257,385},{2,130,258,386},{3,131,259,387},{4,132,..., dimensions={0} | all-to-all | bytes 1048576 | tf_op jit(solution)/shard_map/all_to_all | solution.py:48
  23.4 5.8 %collective-permute-start = (bf16[16,128,128]{2,1,0:T(8,128)(2,1)S(1)}, bf16[16,128,128]{2,1,0:T(8,128)(2,1)S(1)}, u32[]{:S(2)}, u32[]{:S(2)}) collective-permute-start(bf16[16,128,128]{2,1,0:T(8,128)(2,1)S(1)} %bitcast.7), channel_id=1, source_target_pairs={{0,16},{1,17},{2,18},{3,19},{4,20},{5,21},{6,22},{7,23},{8,24},{9,... | collective-permute-start | bytes 1572872 | tf_op jit(solution)/shard_map/ppermute | solution.py:40
  29.1 1.5 %collective-permute-done.other = bf16[16,128,128]{2,1,0:T(8,128)(2,1)S(1)} collective-permute-done((bf16[16,128,128]{2,1,0:T(8,128)(2,1)S(1)}, bf16[16,128,128]{2,1,0:T(8,128)(2,1)S(1)}, u32[]{:S(2)}, u32[]{:S(2)}) %collective-permute-start) | collective-permute-done | bytes 524320 | tf_op jit(solution)/shard_map/ppermute | solution.py:40
  30.6 0.0 copy-done.4
  30.7 0.0 copy-done.3
  30.7 0.0 copy-done
  30.7 0.0 copy-start.1
  30.7 1.0 shard_map.85
  31.7 12.4 %all_to_all.32.parts = bf16[4,4,128,128]{3,2,1,0:T(8,128)(2,1)S(1)} all-to-all(bf16[4,4,128,128]{3,2,1,0:T(8,128)(2,1)S(1)} %get-tuple-element.15), channel_id=1, replica_groups={{0,4,8,12},{1,5,9,13},{2,6,10,14},{3,7,11,15},{16,20,24,28},{17,21,25,2..., dimensions={0} | all-to-all | bytes 1048576 | tf_op jit(solution)/shard_map/all_to_all | solution.py:48
  44.1 0.0 copy-start.2
  44.1 0.0 copy-done.1
  44.1 0.1 shard_map.86
  44.2 30.3 %all-gather = bf16[20,128,128]{2,1,0:T(8,128)(2,1)S(1)} all-gather(bf16[5,128,128]{2,1,0:T(8,128)(2,1)S(1)} %shard_map.86), channel_id=2, replica_groups={{0,1,2,3},{4,5,6,7},{8,9,10,11},{12,13,14,15},{16,17,18,19},{20,21,22,2..., dimensions={0}, use_global_device_ids=true | all-gather | bytes 819200 | tf_op jit(solution)/shard_map/all_gather | solution.py:44
  74.5 0.0 copy-done.2
  74.5 0.9 shard_map.87
  75.4 10.0 %all_to_all.33.parts = bf16[4,5,128,128]{3,2,1,0:T(8,128)(2,1)S(1)} all-to-all(bf16[4,5,128,128]{3,2,1,0:T(8,128)(2,1)S(1)} %get-tuple-element.18), channel_id=1, replica_groups={{0,4,8,12},{1,5,9,13},{2,6,10,14},{3,7,11,15},{16,20,24,28},{17,21,25,2..., dimensions={0} | all-to-all | bytes 1310720 | tf_op jit(solution)/shard_map/all_to_all | solution.py:48
  85.4 1.1 shard_map.88
  86.5 9.1 %collective-permute-start.1 = (f32[2112,128]{1,0:T(8,128)S(1)}, f32[2112,128]{1,0:T(8,128)S(1)}, u32[]{:S(2)}, u32[]{:S(2)}) collective-permute-start(f32[2112,128]{1,0:T(8,128)S(1)} %get-tuple-element.20), channel_id=1, source_target_pairs={{0,16},{1,17},{2,18},{3,19},{4,20},{5,21},{6,22},{7,23},{8,24},{9,... | collective-permute-start | bytes 3244040 | tf_op jit(solution)/shard_map/ppermute | solution.py:40
  95.6 2.3 %collective-permute-done.1.got = f32[2112,128]{1,0:T(8,128)S(1)} collective-permute-done((f32[2112,128]{1,0:T(8,128)S(1)}, f32[2112,128]{1,0:T(8,128)S(1)}, u32[]{:S(2)}, u32[]{:S(2)}) %collective-permute-start.1) | collective-permute-done | bytes 1081376 | tf_op jit(solution)/shard_map/ppermute | solution.py:40
  97.9 0.2 shard_map.89
  98.1 13.0 %all_to_all.34.parts = bf16[4,5,128,128]{3,2,1,0:T(8,128)(2,1)S(1)} all-to-all(bf16[4,5,128,128]{3,2,1,0:T(8,128)(2,1)S(1)} %get-tuple-element.21), channel_id=1, replica_groups={{0,128,256,384},{1,129,257,385},{2,130,258,386},{3,131,259,387},{4,132,..., dimensions={0} | all-to-all | bytes 1310720 | tf_op jit(solution)/shard_map/all_to_all | solution.py:48
  111.2 0.1 shard_map.90
  111.3 10.0 %all_to_all.35.parts = bf16[4,2,128,128]{3,2,1,0:T(8,128)(2,1)S(1)} all-to-all(bf16[4,2,128,128]{3,2,1,0:T(8,128)(2,1)S(1)} %get-tuple-element.23), channel_id=1, replica_groups={{0,32,64,96},{1,33,65,97},{2,34,66,98},{3,35,67,99},{4,36,68,100},{5,37..., dimensions={0} | all-to-all | bytes 524288 | tf_op jit(solution)/shard_map/all_to_all | solution.py:48
  121.2 0.7 shard_map.91
  121.9 5.6 %collective-permute-start.2 = (f32[64,128]{1,0:T(8,128)S(1)}, f32[64,128]{1,0:T(8,128)S(1)}, u32[]{:S(2)}, u32[]{:S(2)}) collective-permute-start(f32[64,128]{1,0:T(8,128)S(1)} %get-tuple-element.26.half), channel_id=1, source_target_pairs={{0,16},{1,17},{2,18},{3,19},{4,20},{5,21},{6,22},{7,23},{8,24},{9,... | collective-permute-start | bytes 98312 | tf_op jit(solution)/shard_map/ppermute | solution.py:40
  127.5 0.8 collective-permute-done.2.got
  128.3 0.6 shard_map.92
Async XLA Ops:
  0.6 30.0 %copy-start.4 = (s32[1,1,16]{2,1,0:T(1,128)S(1)}, s32[1,1,16]{2,1,0:T(1,128)}, u32[]{:S(2)}) copy-start(s32[1,1,16]{2,1,0:T(1,128)} %param.10) | copy-start | bytes 196
  0.6 30.0 %copy-start.3 = (s32[1,1,16]{2,1,0:T(1,128)S(1)}, s32[1,1,16]{2,1,0:T(1,128)}, u32[]{:S(2)}) copy-start(s32[1,1,16]{2,1,0:T(1,128)} %param.9) | copy-start | bytes 196
  0.7 30.0 %copy-start = (bf16[1,1,16,128,128]{4,3,2,1,0:T(8,128)(2,1)S(1)}, bf16[1,1,16,128,128]{4,3,2,1,0:T(8,128)(2,1)}, u32[]{:S(2)}) copy-start(bf16[1,1,16,128,128]{4,3,2,1,0:T(8,128)(2,1)} %param.8) | copy-start | bytes 1572868
  23.4 7.3 %collective-permute-start = (bf16[16,128,128]{2,1,0:T(8,128)(2,1)S(1)}, bf16[16,128,128]{2,1,0:T(8,128)(2,1)S(1)}, u32[]{:S(2)}, u32[]{:S(2)}) collective-permute-start(bf16[16,128,128]{2,1,0:T(8,128)(2,1)S(1)} %bitcast.7), channel_id=1, source_target_pairs={{0,16},{1,17},{2,18},{3,19},{4,20},{5,21},{6,22},{7,23},{8,24},{9,... | collective-permute-start | bytes 1572872 | tf_op jit(solution)/shard_map/ppermute | solution.py:40
  30.7 13.4 %copy-start.1 = (bf16[128,128]{1,0:T(8,128)(2,1)S(1)}, bf16[128,128]{1,0:T(8,128)(2,1)}, u32[]{:S(2)}) copy-start(bf16[128,128]{1,0:T(8,128)(2,1)} %cot.1) | copy-start | bytes 98308
  44.1 30.4 %copy-start.2 = (bf16[128,128]{1,0:T(8,128)(2,1)S(1)}, bf16[128,128]{1,0:T(8,128)(2,1)}, u32[]{:S(2)}) copy-start(bf16[128,128]{1,0:T(8,128)(2,1)} %weight.1) | copy-start | bytes 98308
  86.5 11.4 %collective-permute-start.1 = (f32[2112,128]{1,0:T(8,128)S(1)}, f32[2112,128]{1,0:T(8,128)S(1)}, u32[]{:S(2)}, u32[]{:S(2)}) collective-permute-start(f32[2112,128]{1,0:T(8,128)S(1)} %get-tuple-element.20), channel_id=1, source_target_pairs={{0,16},{1,17},{2,18},{3,19},{4,20},{5,21},{6,22},{7,23},{8,24},{9,... | collective-permute-start | bytes 3244040 | tf_op jit(solution)/shard_map/ppermute | solution.py:40
  121.9 6.4 %collective-permute-start.2 = (f32[64,128]{1,0:T(8,128)S(1)}, f32[64,128]{1,0:T(8,128)S(1)}, u32[]{:S(2)}, u32[]{:S(2)}) collective-permute-start(f32[64,128]{1,0:T(8,128)S(1)} %get-tuple-element.26.half), channel_id=1, source_target_pairs={{0,16},{1,17},{2,18},{3,19},{4,20},{5,21},{6,22},{7,23},{8,24},{9,... | collective-permute-start | bytes 98312 | tf_op jit(solution)/shard_map/ppermute | solution.py:40

commit v4 on v3

--- a/solution.py
+++ b/solution.py
@@ -135,7 +135,7 @@
         out[k, 4] = grad
 
 
-def backward_tiles(rows, cols, adj, parts, keep, send, acc, total):
+def backward_tiles(rows, cols, adj, parts, keep, send, acc):
     core = core_place()
     acc[...] = jnp.zeros_like(acc)
     for t in range(16):
@@ -146,54 +146,49 @@
     grad = parts[0, 4].astype(F32)
     for k in range(1, 4):
         grad += parts[k, 4].astype(F32)
-    total[...] = grad.reshape(2, 64, F)
-    for ref, c in ((keep, core), (send, 1 - core)):
-        ref[pl.ds(0, 2048), :] = acc[c].reshape(2048, F)
-        ref[pl.ds(2048, 64), :] = total[c]
+    high, low = split(grad)
+    keep[pl.ds(0, 16)] = acc[core]
+    send[pl.ds(0, 16)] = acc[1 - core].astype(BF)
+    keep[16] = high.astype(F32) + low.astype(F32)
+    send[16] = high
+    send[17] = low
 
 
 def add_cores(keep, got, out, mine):
-    total = (keep[pl.ds(0, 2048), :] + got[pl.ds(0, 2048), :]).reshape(4, 4, T, F)
-    high, low = split(keep[pl.ds(2048, 64), :] + got[pl.ds(2048, 64), :])
+    high, low = split(keep[16] + (got[16].astype(F32) + got[17].astype(F32)))
     for k in range(4):
-        out[k, pl.ds(0, 4)] = total[k].astype(BF)
-        out[k, 4, pl.ds(0, 64), :] = high
-        out[k, 4, pl.ds(64, 64), :] = low
-    start = pl.multiple_of(x_place() * 512, 512)
-    own = keep[pl.ds(start, 512), :] + got[pl.ds(start, 512), :]
-    mine[...] = own.reshape(4, T, F)
-
-
-def sum_halves(parts, spot):
-    total = parts[0, spot].astype(F32)
+        total = keep[pl.ds(4 * k, 4)] + got[pl.ds(4 * k, 4)].astype(F32)
+        out[k, pl.ds(0, 4)] = total.astype(BF)
+        out[k, 4] = high
+        out[k, 5] = low
+    start = x_place() * 4
+    mine[...] = keep[pl.ds(start, 4)] + got[pl.ds(start, 4)].astype(F32)
+
+
+def sum_grad(parts, spot):
+    total = parts[0, spot].astype(F32) + parts[0, spot + 1].astype(F32)
     for k in range(1, 4):
-        total += parts[k, spot].astype(F32)
-    return total[:64] + total[64:]
+        total += parts[k, spot].astype(F32) + parts[k, spot + 1].astype(F32)
+    return total
 
 
 def add_x(parts, mine, out, own, kept):
     total = plus_others(mine[...], parts, x_place(), 4)
-    high, low = split(sum_halves(parts, 4))
+    high, low = split(sum_grad(parts, 4))
     for k in range(4):
         out[k, 0] = total[k].astype(BF)
-        out[k, 1, pl.ds(0, 64), :] = high
-        out[k, 1, pl.ds(64, 64), :] = low
+        out[k, 1] = high
+        out[k, 2] = low
     kept[...] = total
     own[...] = kept[zl_place()]
 
 
-def add_z(parts, own, out, half):
+def add_z(parts, own, out, grad):
     total = own[...]
     for j in range(1, 4):
         total += parts[lax.rem(zl_place() + j, 4), 0].astype(F32)
     out[...] = total
-    half[...] = sum_halves(parts, 1)
-
-
-def join(half, got, grad):
-    core = core_place()
-    grad[core] = half[...]
-    grad[1 - core] = got[...]
+    grad[...] = sum_grad(parts, 1)
 
 
 def per_device(features, weight, adj_values, tile_rows, tile_cols, cotangent):
@@ -219,20 +214,19 @@
     parts = exchange(back, "y")
     keep, send = call(
         backward_tiles,
-        [((2112, F), F32), ((2112, F), F32)],
+        [((17, T, F), F32), ((18, T, F), BF)],
         "ssvv",
-        [pltpu.VMEM((2, 16, T, F), F32), pltpu.VMEM((2, 64, F), F32)],
+        [pltpu.VMEM((2, 16, T, F), F32)],
     )(rows, cols, adj, parts)
     got = swap_core(send)
-    parts, mine = call(add_cores, [((4, 5, T, F), BF), ((4, T, F), F32)], "vv")(keep, got)
+    parts, mine = call(add_cores, [((4, 6, T, F), BF), ((4, T, F), F32)], "vv")(keep, got)
     parts = exchange(parts, "x")
     parts, own = call(
-        add_x, [((4, 2, T, F), BF), (tile, F32)], "vv", [pltpu.VMEM((4, T, F), F32)]
+        add_x, [((4, 3, T, F), BF), (tile, F32)], "vv", [pltpu.VMEM((4, T, F), F32)]
     )(parts, mine)
     parts = exchange(parts, "zl")
-    out, half = call(add_z, [(tile, F32), ((64, F), F32)], "vv")(parts, own)
-    (grad,) = call(join, [((2, 64, F), F32)], "vv")(half, swap_core(half))
-    return act, out, grad.reshape(F, F)
+    out, grad = call(add_z, [(tile, F32), (tile, F32)], "vv")(parts, own)
+    return act, out, grad
 
 
 def solution(mesh):

time: 130 us -> 127 us (0.977)
  blocking collectives: 97.5 us -> 104 us
  starting transfers between devices: 20.4 us -> 14.5 us
  waiting for transfers between devices: 4.66 us -> 3.12 us
    all_to_all x6, blocking collectives: 67.2 us -> 73.1 us  [exchange(): lax.all_to_all(array, BOTH, 0, 0, tiled=True, axis_index_groups=groups(ax...]
    ppermute x3 -> x2, starting transfers between devices: 20.4 us -> 14.5 us  [swap_core(): return lax.ppermute(array, BOTH, pairs)]
    ppermute x3 -> x2, waiting for transfers between devices: 4.66 us -> 3.12 us  [swap_core(): return lax.ppermute(array, BOTH, pairs)]
    pallas_call x5 -> x4, Pallas kernels: 2.78 us -> 2.11 us  [the longest x1 1.13 us: per_device(): call(backward_tiles, [((17, T, F), F32), ((18, T, F), BF)], 'ssvv', [pltp...]
  transfers between devices with their start and end apart: 3 -> 2, of which waited for: 3 -> 2; matrix products, arithmetic and copies ran while one was open for 0% -> 0% of each run, Pallas kernels for 0% -> 0%
where the time goes in v4:
time: 127 us
  blocking collectives  104 us (82%)
  starting transfers between devices  14.5 us (11%)
  Pallas kernels  4.06 us (3%)
  waiting for transfers between devices  3.12 us (2%)
    all_to_all x6, blocking collectives, exchange(): lax.all_to_all(array, BOTH, 0, 0, tiled=True, axis_index_groups=groups(ax...  73.1 us
    all_gather x1, blocking collectives, gather(): lax.all_gather(array, BOTH, axis=0, tiled=False, axis_index_groups=groups...  30.4 us
    ppermute x2, starting transfers between devices, swap_core(): return lax.ppermute(array, BOTH, pairs)  14.5 us
    ppermute x2, waiting for transfers between devices, swap_core(): return lax.ppermute(array, BOTH, pairs)  3.12 us
  transfers between devices with their start and end apart: 2, of which 2 were waited for; matrix products, arithmetic and copies ran while one was open for 0% of the time, Pallas kernels for 0%

profile of v4, /device:TPU:1, one launch (start us, length us, event | category | flops | bytes accessed | tf_op | source)
XLA Modules:
  0.0 126.9 jit_solution(14107595931432022477)
XLA Ops:
  0.6 0.0 copy-start.4
  0.6 0.0 copy-start.3
  0.7 0.0 copy-start
  0.7 0.8 broadcast_in_dim.4
  1.5 11.0 %all_to_all.30 = bf16[4,128,128]{2,1,0:T(8,128)(2,1)S(1)} all-to-all(bf16[4,128,128]{2,1,0:T(8,128)(2,1)S(1)} %broadcast_in_dim.4), channel_id=1, replica_groups={{0,32,64,96},{1,33,65,97},{2,34,66,98},{3,35,67,99},{4,36,68,100},{5,37..., dimensions={0} | all-to-all | bytes 262144 | tf_op jit(solution)/shard_map/all_to_all | solution.py:48
  12.5 0.1 broadcast_in_dim.5
  12.6 10.7 %all_to_all.31 = bf16[4,4,128,128]{3,2,1,0:T(8,128)(2,1)S(1)} all-to-all(bf16[4,4,128,128]{3,2,1,0:T(8,128)(2,1)S(1)} %broadcast_in_dim.5), channel_id=1, replica_groups={{0,128,256,384},{1,129,257,385},{2,130,258,386},{3,131,259,387},{4,132,..., dimensions={0} | all-to-all | bytes 1048576 | tf_op jit(solution)/shard_map/all_to_all | solution.py:48
  23.4 5.8 %collective-permute-start = (bf16[16,128,128]{2,1,0:T(8,128)(2,1)S(1)}, bf16[16,128,128]{2,1,0:T(8,128)(2,1)S(1)}, u32[]{:S(2)}, u32[]{:S(2)}) collective-permute-start(bf16[16,128,128]{2,1,0:T(8,128)(2,1)S(1)} %bitcast.6), channel_id=1, source_target_pairs={{0,16},{1,17},{2,18},{3,19},{4,20},{5,21},{6,22},{7,23},{8,24},{9,... | collective-permute-start | bytes 1572872 | tf_op jit(solution)/shard_map/ppermute | solution.py:40
  29.1 1.5 %collective-permute-done.other = bf16[16,128,128]{2,1,0:T(8,128)(2,1)S(1)} collective-permute-done((bf16[16,128,128]{2,1,0:T(8,128)(2,1)S(1)}, bf16[16,128,128]{2,1,0:T(8,128)(2,1)S(1)}, u32[]{:S(2)}, u32[]{:S(2)}) %collective-permute-start) | collective-permute-done | bytes 524320 | tf_op jit(solution)/shard_map/ppermute | solution.py:40
  30.6 0.0 copy-done.4
  30.7 0.0 copy-done.3
  30.7 0.0 copy-done
  30.7 0.0 copy-start.1
  30.7 1.0 shard_map.85
  31.7 12.4 %all_to_all.32.parts = bf16[4,4,128,128]{3,2,1,0:T(8,128)(2,1)S(1)} all-to-all(bf16[4,4,128,128]{3,2,1,0:T(8,128)(2,1)S(1)} %get-tuple-element.15), channel_id=1, replica_groups={{0,4,8,12},{1,5,9,13},{2,6,10,14},{3,7,11,15},{16,20,24,28},{17,21,25,2..., dimensions={0} | all-to-all | bytes 1048576 | tf_op jit(solution)/shard_map/all_to_all | solution.py:48
  44.1 0.0 copy-start.2
  44.1 0.0 copy-done.1
  44.1 0.1 shard_map.86
  44.2 30.4 %all-gather = bf16[20,128,128]{2,1,0:T(8,128)(2,1)S(1)} all-gather(bf16[5,128,128]{2,1,0:T(8,128)(2,1)S(1)} %shard_map.86), channel_id=2, replica_groups={{0,1,2,3},{4,5,6,7},{8,9,10,11},{12,13,14,15},{16,17,18,19},{20,21,22,2..., dimensions={0}, use_global_device_ids=true | all-gather | bytes 819200 | tf_op jit(solution)/shard_map/all_gather | solution.py:44
  74.6 0.0 copy-done.2
  74.6 0.9 shard_map.87
  75.5 10.0 %all_to_all.33.parts = bf16[4,5,128,128]{3,2,1,0:T(8,128)(2,1)S(1)} all-to-all(bf16[4,5,128,128]{3,2,1,0:T(8,128)(2,1)S(1)} %get-tuple-element.18), channel_id=1, replica_groups={{0,4,8,12},{1,5,9,13},{2,6,10,14},{3,7,11,15},{16,20,24,28},{17,21,25,2..., dimensions={0} | all-to-all | bytes 1310720 | tf_op jit(solution)/shard_map/all_to_all | solution.py:48
  85.5 1.1 shard_map.88
  86.7 8.7 %collective-permute-start.1 = (bf16[18,128,128]{2,1,0:T(8,128)(2,1)S(1)}, bf16[18,128,128]{2,1,0:T(8,128)(2,1)S(1)}, u32[]{:S(2)}, u32[]{:S(2)}) collective-permute-start(bf16[18,128,128]{2,1,0:T(8,128)(2,1)S(1)} %get-tuple-element.20), channel_id=1, source_target_pairs={{0,16},{1,17},{2,18},{3,19},{4,20},{5,21},{6,22},{7,23},{8,24},{9,... | collective-permute-start | bytes 1769480 | tf_op jit(solution)/shard_map/ppermute | solution.py:40
  95.4 1.6 %collective-permute-done.1.got = bf16[18,128,128]{2,1,0:T(8,128)(2,1)S(1)} collective-permute-done((bf16[18,128,128]{2,1,0:T(8,128)(2,1)S(1)}, bf16[18,128,128]{2,1,0:T(8,128)(2,1)S(1)}, u32[]{:S(2)}, u32[]{:S(2)}) %collective-permute-start.1) | collective-permute-done | bytes 589856 | tf_op jit(solution)/shard_map/ppermute | solution.py:40
  97.0 0.2 shard_map.89
  97.2 14.4 %all_to_all.34.parts = bf16[4,6,128,128]{3,2,1,0:T(8,128)(2,1)S(1)} all-to-all(bf16[4,6,128,128]{3,2,1,0:T(8,128)(2,1)S(1)} %get-tuple-element.21), channel_id=1, replica_groups={{0,128,256,384},{1,129,257,385},{2,130,258,386},{3,131,259,387},{4,132,..., dimensions={0} | all-to-all | bytes 1572864 | tf_op jit(solution)/shard_map/all_to_all | solution.py:48
  111.6 0.1 shard_map.90
  111.7 14.5 %all_to_all.35.parts = bf16[4,3,128,128]{3,2,1,0:T(8,128)(2,1)S(1)} all-to-all(bf16[4,3,128,128]{3,2,1,0:T(8,128)(2,1)S(1)} %get-tuple-element.23), channel_id=1, replica_groups={{0,32,64,96},{1,33,65,97},{2,34,66,98},{3,35,67,99},{4,36,68,100},{5,37..., dimensions={0} | all-to-all | bytes 786432 | tf_op jit(solution)/shard_map/all_to_all | solution.py:48
  126.2 0.7 shard_map.91
Async XLA Ops:
  0.6 30.0 %copy-start.4 = (s32[1,1,16]{2,1,0:T(1,128)S(1)}, s32[1,1,16]{2,1,0:T(1,128)}, u32[]{:S(2)}) copy-start(s32[1,1,16]{2,1,0:T(1,128)} %param.10) | copy-start | bytes 196
  0.6 30.0 %copy-start.3 = (s32[1,1,16]{2,1,0:T(1,128)S(1)}, s32[1,1,16]{2,1,0:T(1,128)}, u32[]{:S(2)}) copy-start(s32[1,1,16]{2,1,0:T(1,128)} %param.9) | copy-start | bytes 196
  0.7 30.0 %copy-start = (bf16[1,1,16,128,128]{4,3,2,1,0:T(8,128)(2,1)S(1)}, bf16[1,1,16,128,128]{4,3,2,1,0:T(8,128)(2,1)}, u32[]{:S(2)}) copy-start(bf16[1,1,16,128,128]{4,3,2,1,0:T(8,128)(2,1)} %param.8) | copy-start | bytes 1572868
  23.4 7.3 %collective-permute-start = (bf16[16,128,128]{2,1,0:T(8,128)(2,1)S(1)}, bf16[16,128,128]{2,1,0:T(8,128)(2,1)S(1)}, u32[]{:S(2)}, u32[]{:S(2)}) collective-permute-start(bf16[16,128,128]{2,1,0:T(8,128)(2,1)S(1)} %bitcast.6), channel_id=1, source_target_pairs={{0,16},{1,17},{2,18},{3,19},{4,20},{5,21},{6,22},{7,23},{8,24},{9,... | collective-permute-start | bytes 1572872 | tf_op jit(solution)/shard_map/ppermute | solution.py:40
  30.7 13.4 %copy-start.1 = (bf16[128,128]{1,0:T(8,128)(2,1)S(1)}, bf16[128,128]{1,0:T(8,128)(2,1)}, u32[]{:S(2)}) copy-start(bf16[128,128]{1,0:T(8,128)(2,1)} %cot.1) | copy-start | bytes 98308
  44.1 30.5 %copy-start.2 = (bf16[128,128]{1,0:T(8,128)(2,1)S(1)}, bf16[128,128]{1,0:T(8,128)(2,1)}, u32[]{:S(2)}) copy-start(bf16[128,128]{1,0:T(8,128)(2,1)} %weight.1) | copy-start | bytes 98308
  86.7 10.4 %collective-permute-start.1 = (bf16[18,128,128]{2,1,0:T(8,128)(2,1)S(1)}, bf16[18,128,128]{2,1,0:T(8,128)(2,1)S(1)}, u32[]{:S(2)}, u32[]{:S(2)}) collective-permute-start(bf16[18,128,128]{2,1,0:T(8,128)(2,1)S(1)} %get-tuple-element.20), channel_id=1, source_target_pairs={{0,16},{1,17},{2,18},{3,19},{4,20},{5,21},{6,22},{7,23},{8,24},{9,... | collective-permute-start | bytes 1769480 | tf_op jit(solution)/shard_map/ppermute | solution.py:40

commit v5 on v4

--- a/solution.py
+++ b/solution.py
@@ -27,10 +27,10 @@
         yield dict(zip(SIZES, values))
 
 
-def groups(axis):
+def groups(*axes):
     found = {}
     for place in places():
-        key = tuple(v for n, v in place.items() if n != axis)
+        key = tuple(v for n, v in place.items() if n not in axes)
         found.setdefault(key, []).append(position(place))
     return list(found.values())
 
@@ -44,12 +44,8 @@
     return lax.all_gather(array, BOTH, axis=0, tiled=False, axis_index_groups=groups(axis))
 
 
-def exchange(array, axis):
-    return lax.all_to_all(array, BOTH, 0, 0, tiled=True, axis_index_groups=groups(axis))
-
-
-def spread(array):
-    return jnp.broadcast_to(array[None], (4, *array.shape))
+def exchange(array, *axes):
+    return lax.all_to_all(array, BOTH, 0, 0, tiled=True, axis_index_groups=groups(*axes))
 
 
 def core_place():
@@ -129,10 +125,11 @@
     cot = jnp.concatenate([parts[k, 4] for k in range(4)], axis=0)
     dpre = (cot.astype(F32) * sig * (1.0 + pre * (1.0 - sig))).astype(BF)
     back = dot(dpre, w, ((1,), (1,))).astype(BF).reshape(4, T, F)
-    grad = dot(zed, dpre, ((0,), (0,))).astype(BF)
+    high, low = split(dot(zed, dpre, ((0,), (0,))))
     for k in range(4):
         out[k, pl.ds(0, 4)] = back
-        out[k, 4] = grad
+        out[k, 4] = high
+        out[k, 5] = low
 
 
 def backward_tiles(rows, cols, adj, parts, keep, send, acc):
@@ -143,10 +140,7 @@
         b = cols[t]
         d = parts[lax.div(r, 4), lax.rem(r, 4)]
         acc[lax.rem(b, 2), lax.div(b, 2)] += dot(adj[t], d, ((0,), (0,)))
-    grad = parts[0, 4].astype(F32)
-    for k in range(1, 4):
-        grad += parts[k, 4].astype(F32)
-    high, low = split(grad)
+    high, low = split(sum_grad(parts, 4))
     keep[pl.ds(0, 16)] = acc[core]
     send[pl.ds(0, 16)] = acc[1 - core].astype(BF)
     keep[16] = high.astype(F32) + low.astype(F32)
@@ -174,11 +168,10 @@
 
 def add_x(parts, mine, out, own, kept):
     total = plus_others(mine[...], parts, x_place(), 4)
-    high, low = split(sum_grad(parts, 4))
+    grad = sum_grad(parts, 4).astype(BF)
     for k in range(4):
         out[k, 0] = total[k].astype(BF)
-        out[k, 1] = high
-        out[k, 2] = low
+        out[k, 1] = grad
     kept[...] = total
     own[...] = kept[zl_place()]
 
@@ -188,7 +181,10 @@
     for j in range(1, 4):
         total += parts[lax.rem(zl_place() + j, 4), 0].astype(F32)
     out[...] = total
-    grad[...] = sum_grad(parts, 1)
+    total = parts[0, 1].astype(F32)
+    for k in range(1, 4):
+        total += parts[k, 1].astype(F32)
+    grad[...] = total
 
 
 def per_device(features, weight, adj_values, tile_rows, tile_cols, cotangent):
@@ -197,7 +193,7 @@
     cols = tile_cols.reshape(16)
     tile = (T, F)
 
-    own = exchange(spread(exchange(spread(features), "zl")), "x").reshape(16, T, F)
+    own = exchange(jnp.broadcast_to(features[None], (16, T, F)), "x", "zl")
     other = swap_core(own)
     partial, mine = call(
         forward_tiles,
@@ -209,7 +205,7 @@
     (summed,) = call(add_y, [((5, T, F), BF)], "vvv")(parts, mine, cotangent)
     parts = gather(summed, "zh")
     act, back = call(
-        layer, [(tile, F32), ((4, 5, T, F), BF)], "vv", [pltpu.VMEM((4, T, F), F32)]
+        layer, [(tile, F32), ((4, 6, T, F), BF)], "vv", [pltpu.VMEM((4, T, F), F32)]
     )(parts, weight)
     parts = exchange(back, "y")
     keep, send = call(
@@ -222,7 +218,7 @@
     parts, mine = call(add_cores, [((4, 6, T, F), BF), ((4, T, F), F32)], "vv")(keep, got)
     parts = exchange(parts, "x")
     parts, own = call(
-        add_x, [((4, 3, T, F), BF), (tile, F32)], "vv", [pltpu.VMEM((4, T, F), F32)]
+        add_x, [((4, 2, T, F), BF), (tile, F32)], "vv", [pltpu.VMEM((4, T, F), F32)]
     )(parts, mine)
     parts = exchange(parts, "zl")
     out, grad = call(add_z, [(tile, F32), (tile, F32)], "vv")(parts, own)

time: 127 us -> 126 us (level)
  starting transfers between devices: 14.5 us -> 7.34 us
  blocking collectives: 104 us -> 109 us
    ppermute x2, starting transfers between devices: 14.5 us -> 7.34 us  [swap_core(): return lax.ppermute(array, BOTH, pairs)]
    all_gather x1, blocking collectives: 30.4 us -> 34.7 us  [gather(): lax.all_gather(array, BOTH, axis=0, tiled=False, axis_index_groups=groups...]
    all_to_all x6 -> x5, blocking collectives: 73.1 us -> 73.9 us  [exchange(): lax.all_to_all(array, BOTH, 0, 0, tiled=True, axis_index_groups=groups(*a...]
where the time goes in v5:
time: 126 us; the launch traced here: 125 us
  blocking collectives  109 us (87%)
  starting transfers between devices  7.34 us (6%)
  Pallas kernels  4.05 us (3%)
  waiting for transfers between devices  3.12 us (2%)
    all_to_all x5, blocking collectives, exchange(): lax.all_to_all(array, BOTH, 0, 0, tiled=True, axis_index_groups=groups(*a...  73.9 us
    all_gather x1, blocking collectives, gather(): lax.all_gather(array, BOTH, axis=0, tiled=False, axis_index_groups=groups...  34.7 us
    ppermute x2, starting transfers between devices, swap_core(): return lax.ppermute(array, BOTH, pairs)  7.34 us
    ppermute x2, waiting for transfers between devices, swap_core(): return lax.ppermute(array, BOTH, pairs)  3.12 us
  transfers between devices with their start and end apart: 2, of which 2 were waited for; matrix products, arithmetic and copies ran while one was open for 0% of the time, Pallas kernels for 0%

profile of v5, /device:TPU:1, one launch (start us, length us, event | category | flops | bytes accessed | tf_op | source)
XLA Modules:
  0.0 124.9 jit_solution(3096779257356540718)
XLA Ops:
  0.6 0.0 copy-start.4
  0.6 0.0 copy-start.3
  0.7 0.0 copy-start
  0.7 0.9 broadcast_in_dim.2
  1.6 24.6 %all_to_all.25.own = bf16[16,128,128]{2,1,0:T(8,128)(2,1)S(1)} all-to-all(bf16[16,128,128]{2,1,0:T(8,128)(2,1)S(1)} %broadcast_in_dim.2), channel_id=1, replica_groups={{0,32,64,96,128,160,192,224,256,288,320,352,384,416,448,480},{1,33,65,9..., dimensions={0} | all-to-all | bytes 1048576 | tf_op jit(solution)/shard_map/all_to_all | solution.py:48
  26.2 3.6 %collective-permute-start = (bf16[16,128,128]{2,1,0:T(8,128)(2,1)S(1)}, bf16[16,128,128]{2,1,0:T(8,128)(2,1)S(1)}, u32[]{:S(2)}, u32[]{:S(2)}) collective-permute-start(bf16[16,128,128]{2,1,0:T(8,128)(2,1)S(1)} %all_to_all.25.own), channel_id=1, source_target_pairs={{0,16},{1,17},{2,18},{3,19},{4,20},{5,21},{6,22},{7,23},{8,24},{9,... | collective-permute-start | bytes 1572872 | tf_op jit(solution)/shard_map/ppermute | solution.py:40
  29.7 1.5 %collective-permute-done.other = bf16[16,128,128]{2,1,0:T(8,128)(2,1)S(1)} collective-permute-done((bf16[16,128,128]{2,1,0:T(8,128)(2,1)S(1)}, bf16[16,128,128]{2,1,0:T(8,128)(2,1)S(1)}, u32[]{:S(2)}, u32[]{:S(2)}) %collective-permute-start) | collective-permute-done | bytes 524320 | tf_op jit(solution)/shard_map/ppermute | solution.py:40
  31.3 0.0 copy-done.4
  31.3 0.0 copy-done.3
  31.3 0.0 copy-done
  31.3 0.0 copy-start.1
  31.3 1.0 shard_map.85
  32.3 12.6 %all_to_all.26.parts = bf16[4,4,128,128]{3,2,1,0:T(8,128)(2,1)S(1)} all-to-all(bf16[4,4,128,128]{3,2,1,0:T(8,128)(2,1)S(1)} %get-tuple-element.15), channel_id=1, replica_groups={{0,4,8,12},{1,5,9,13},{2,6,10,14},{3,7,11,15},{16,20,24,28},{17,21,25,2..., dimensions={0} | all-to-all | bytes 1048576 | tf_op jit(solution)/shard_map/all_to_all | solution.py:48
  44.9 0.0 copy-start.2
  44.9 0.0 copy-done.1
  44.9 0.1 shard_map.86
  45.0 34.7 %all-gather = bf16[20,128,128]{2,1,0:T(8,128)(2,1)S(1)} all-gather(bf16[5,128,128]{2,1,0:T(8,128)(2,1)S(1)} %shard_map.86), channel_id=2, replica_groups={{0,1,2,3},{4,5,6,7},{8,9,10,11},{12,13,14,15},{16,17,18,19},{20,21,22,2..., dimensions={0}, use_global_device_ids=true | all-gather | bytes 819200 | tf_op jit(solution)/shard_map/all_gather | solution.py:44
  79.7 0.0 copy-done.2
  79.7 0.9 shard_map.87
  80.6 13.8 %all_to_all.27.parts = bf16[4,6,128,128]{3,2,1,0:T(8,128)(2,1)S(1)} all-to-all(bf16[4,6,128,128]{3,2,1,0:T(8,128)(2,1)S(1)} %get-tuple-element.18), channel_id=1, replica_groups={{0,4,8,12},{1,5,9,13},{2,6,10,14},{3,7,11,15},{16,20,24,28},{17,21,25,2..., dimensions={0} | all-to-all | bytes 1572864 | tf_op jit(solution)/shard_map/all_to_all | solution.py:48
  94.4 1.1 shard_map.88
  95.5 3.8 %collective-permute-start.1 = (bf16[18,128,128]{2,1,0:T(8,128)(2,1)S(1)}, bf16[18,128,128]{2,1,0:T(8,128)(2,1)S(1)}, u32[]{:S(2)}, u32[]{:S(2)}) collective-permute-start(bf16[18,128,128]{2,1,0:T(8,128)(2,1)S(1)} %get-tuple-element.20), channel_id=1, source_target_pairs={{0,16},{1,17},{2,18},{3,19},{4,20},{5,21},{6,22},{7,23},{8,24},{9,... | collective-permute-start | bytes 1769480 | tf_op jit(solution)/shard_map/ppermute | solution.py:40
  99.3 1.6 %collective-permute-done.1.got = bf16[18,128,128]{2,1,0:T(8,128)(2,1)S(1)} collective-permute-done((bf16[18,128,128]{2,1,0:T(8,128)(2,1)S(1)}, bf16[18,128,128]{2,1,0:T(8,128)(2,1)S(1)}, u32[]{:S(2)}, u32[]{:S(2)}) %collective-permute-start.1) | collective-permute-done | bytes 589856 | tf_op jit(solution)/shard_map/ppermute | solution.py:40
  100.9 0.2 shard_map.89
  101.1 14.4 %all_to_all.28.parts = bf16[4,6,128,128]{3,2,1,0:T(8,128)(2,1)S(1)} all-to-all(bf16[4,6,128,128]{3,2,1,0:T(8,128)(2,1)S(1)} %get-tuple-element.21), channel_id=1, replica_groups={{0,128,256,384},{1,129,257,385},{2,130,258,386},{3,131,259,387},{4,132,..., dimensions={0} | all-to-all | bytes 1572864 | tf_op jit(solution)/shard_map/all_to_all | solution.py:48
  115.5 0.1 shard_map.90
  115.7 8.5 %all_to_all.29.parts = bf16[4,2,128,128]{3,2,1,0:T(8,128)(2,1)S(1)} all-to-all(bf16[4,2,128,128]{3,2,1,0:T(8,128)(2,1)S(1)} %get-tuple-element.23), channel_id=1, replica_groups={{0,32,64,96},{1,33,65,97},{2,34,66,98},{3,35,67,99},{4,36,68,100},{5,37..., dimensions={0} | all-to-all | bytes 524288 | tf_op jit(solution)/shard_map/all_to_all | solution.py:48
  124.2 0.7 shard_map.91
Async XLA Ops:
  0.6 30.6 %copy-start.4 = (s32[1,1,16]{2,1,0:T(1,128)S(1)}, s32[1,1,16]{2,1,0:T(1,128)}, u32[]{:S(2)}) copy-start(s32[1,1,16]{2,1,0:T(1,128)} %param.10) | copy-start | bytes 196
  0.6 30.6 %copy-start.3 = (s32[1,1,16]{2,1,0:T(1,128)S(1)}, s32[1,1,16]{2,1,0:T(1,128)}, u32[]{:S(2)}) copy-start(s32[1,1,16]{2,1,0:T(1,128)} %param.9) | copy-start | bytes 196
  0.7 30.6 %copy-start = (bf16[1,1,16,128,128]{4,3,2,1,0:T(8,128)(2,1)S(1)}, bf16[1,1,16,128,128]{4,3,2,1,0:T(8,128)(2,1)}, u32[]{:S(2)}) copy-start(bf16[1,1,16,128,128]{4,3,2,1,0:T(8,128)(2,1)} %param.8) | copy-start | bytes 1572868
  26.2 5.1 %collective-permute-start = (bf16[16,128,128]{2,1,0:T(8,128)(2,1)S(1)}, bf16[16,128,128]{2,1,0:T(8,128)(2,1)S(1)}, u32[]{:S(2)}, u32[]{:S(2)}) collective-permute-start(bf16[16,128,128]{2,1,0:T(8,128)(2,1)S(1)} %all_to_all.25.own), channel_id=1, source_target_pairs={{0,16},{1,17},{2,18},{3,19},{4,20},{5,21},{6,22},{7,23},{8,24},{9,... | collective-permute-start | bytes 1572872 | tf_op jit(solution)/shard_map/ppermute | solution.py:40
  31.3 13.6 %copy-start.1 = (bf16[128,128]{1,0:T(8,128)(2,1)S(1)}, bf16[128,128]{1,0:T(8,128)(2,1)}, u32[]{:S(2)}) copy-start(bf16[128,128]{1,0:T(8,128)(2,1)} %cot.1) | copy-start | bytes 98308
  44.9 34.8 %copy-start.2 = (bf16[128,128]{1,0:T(8,128)(2,1)S(1)}, bf16[128,128]{1,0:T(8,128)(2,1)}, u32[]{:S(2)}) copy-start(bf16[128,128]{1,0:T(8,128)(2,1)} %weight.1) | copy-start | bytes 98308
  95.5 5.4 %collective-permute-start.1 = (bf16[18,128,128]{2,1,0:T(8,128)(2,1)S(1)}, bf16[18,128,128]{2,1,0:T(8,128)(2,1)S(1)}, u32[]{:S(2)}, u32[]{:S(2)}) collective-permute-start(bf16[18,128,128]{2,1,0:T(8,128)(2,1)S(1)} %get-tuple-element.20), channel_id=1, source_target_pairs={{0,16},{1,17},{2,18},{3,19},{4,20},{5,21},{6,22},{7,23},{8,24},{9,... | collective-permute-start | bytes 1769480 | tf_op jit(solution)/shard_map/ppermute | solution.py:40

commit v6 on v5

--- a/solution.py
+++ b/solution.py
@@ -116,16 +116,19 @@
     total = parts[0, pl.ds(0, 4)].astype(F32)
     for k in range(1, 4):
         total += parts[k, pl.ds(0, 4)].astype(F32)
-    zed = total.reshape(512, F).astype(BF)
+    zed, zed_low = split(total.reshape(512, F))
     w = weight[...]
-    pre = dot(zed, w, ((1,), (0,)))
+    pre = dot(zed, w, ((1,), (0,))) + dot(zed_low, w, ((1,), (0,)))
     sig = jax.nn.sigmoid(pre)
     kept[...] = (pre * sig).reshape(4, T, F)
     act[...] = kept[zh_place()]
     cot = jnp.concatenate([parts[k, 4] for k in range(4)], axis=0)
-    dpre = (cot.astype(F32) * sig * (1.0 + pre * (1.0 - sig))).astype(BF)
-    back = dot(dpre, w, ((1,), (1,))).astype(BF).reshape(4, T, F)
-    high, low = split(dot(zed, dpre, ((0,), (0,))))
+    dpre, dpre_low = split(cot.astype(F32) * sig * (1.0 + pre * (1.0 - sig)))
+    back = dot(dpre, w, ((1,), (1,))) + dot(dpre_low, w, ((1,), (1,)))
+    back = back.astype(BF).reshape(4, T, F)
+    rows = ((0,), (0,))
+    grad = dot(zed, dpre, rows) + dot(zed_low, dpre, rows) + dot(zed, dpre_low, rows)
+    high, low = split(grad)
     for k in range(4):
         out[k, pl.ds(0, 4)] = back
         out[k, 4] = high
@@ -140,7 +143,7 @@
         b = cols[t]
         d = parts[lax.div(r, 4), lax.rem(r, 4)]
         acc[lax.rem(b, 2), lax.div(b, 2)] += dot(adj[t], d, ((0,), (0,)))
-    high, low = split(sum_grad(parts, 4))
+    high, low = split(sum_of(parts, 4) + sum_of(parts, 5))
     keep[pl.ds(0, 16)] = acc[core]
     send[pl.ds(0, 16)] = acc[1 - core].astype(BF)
     keep[16] = high.astype(F32) + low.astype(F32)
@@ -149,26 +152,25 @@
 
 
 def add_cores(keep, got, out, mine):
-    high, low = split(keep[16] + (got[16].astype(F32) + got[17].astype(F32)))
+    grad = (keep[16] + (got[16].astype(F32) + got[17].astype(F32))).astype(BF)
     for k in range(4):
         total = keep[pl.ds(4 * k, 4)] + got[pl.ds(4 * k, 4)].astype(F32)
         out[k, pl.ds(0, 4)] = total.astype(BF)
-        out[k, 4] = high
-        out[k, 5] = low
+        out[k, 4] = grad
     start = x_place() * 4
     mine[...] = keep[pl.ds(start, 4)] + got[pl.ds(start, 4)].astype(F32)
 
 
-def sum_grad(parts, spot):
-    total = parts[0, spot].astype(F32) + parts[0, spot + 1].astype(F32)
+def sum_of(parts, spot):
+    total = parts[0, spot].astype(F32)
     for k in range(1, 4):
-        total += parts[k, spot].astype(F32) + parts[k, spot + 1].astype(F32)
+        total += parts[k, spot].astype(F32)
     return total
 
 
 def add_x(parts, mine, out, own, kept):
     total = plus_others(mine[...], parts, x_place(), 4)
-    grad = sum_grad(parts, 4).astype(BF)
+    grad = sum_of(parts, 4).astype(BF)
     for k in range(4):
         out[k, 0] = total[k].astype(BF)
         out[k, 1] = grad
@@ -181,10 +183,7 @@
     for j in range(1, 4):
         total += parts[lax.rem(zl_place() + j, 4), 0].astype(F32)
     out[...] = total
-    total = parts[0, 1].astype(F32)
-    for k in range(1, 4):
-        total += parts[k, 1].astype(F32)
-    grad[...] = total
+    grad[...] = sum_of(parts, 1)
 
 
 def per_device(features, weight, adj_values, tile_rows, tile_cols, cotangent):
@@ -193,7 +192,8 @@
     cols = tile_cols.reshape(16)
     tile = (T, F)
 
-    own = exchange(jnp.broadcast_to(features[None], (16, T, F)), "x", "zl")
+    own = exchange(jnp.broadcast_to(features[None], (4, T, F)), "zl")
+    own = exchange(jnp.broadcast_to(own[None], (4, 4, T, F)), "x").reshape(16, T, F)
     other = swap_core(own)
     partial, mine = call(
         forward_tiles,
@@ -215,7 +215,7 @@
         [pltpu.VMEM((2, 16, T, F), F32)],
     )(rows, cols, adj, parts)
     got = swap_core(send)
-    parts, mine = call(add_cores, [((4, 6, T, F), BF), ((4, T, F), F32)], "vv")(keep, got)
+    parts, mine = call(add_cores, [((4, 5, T, F), BF), ((4, T, F), F32)], "vv")(keep, got)
     parts = exchange(parts, "x")
     parts, own = call(
         add_x, [((4, 2, T, F), BF), (tile, F32)], "vv", [pltpu.VMEM((4, T, F), F32)]

time: 126 us -> 124 us (0.984)
  blocking collectives: 109 us -> 98.9 us
  starting transfers between devices: 7.34 us -> 14.5 us
    ppermute x2, starting transfers between devices: 7.34 us -> 14.5 us  [swap_core(): return lax.ppermute(array, BOTH, pairs)]
    all_to_all x5 -> x6, blocking collectives: 73.9 us -> 68.4 us  [exchange(): lax.all_to_all(array, BOTH, 0, 0, tiled=True, axis_index_groups=groups(*a...]
    all_gather x1, blocking collectives: 34.7 us -> 30.5 us  [gather(): lax.all_gather(array, BOTH, axis=0, tiled=False, axis_index_groups=groups...]
where the time goes in v6:
time: 124 us; the launch traced here: 122 us
  blocking collectives  98.9 us (80%)
  starting transfers between devices  14.5 us (12%)
  Pallas kernels  4.13 us (3%)
  waiting for transfers between devices  3.12 us (3%)
    all_to_all x6, blocking collectives, exchange(): lax.all_to_all(array, BOTH, 0, 0, tiled=True, axis_index_groups=groups(*a...  68.4 us
    all_gather x1, blocking collectives, gather(): lax.all_gather(array, BOTH, axis=0, tiled=False, axis_index_groups=groups...  30.5 us
    ppermute x2, starting transfers between devices, swap_core(): return lax.ppermute(array, BOTH, pairs)  14.5 us
    ppermute x2, waiting for transfers between devices, swap_core(): return lax.ppermute(array, BOTH, pairs)  3.12 us
  transfers between devices with their start and end apart: 2, of which 2 were waited for; matrix products, arithmetic and copies ran while one was open for 0% of the time, Pallas kernels for 0%

profile of v6, /device:TPU:1, one launch (start us, length us, event | category | flops | bytes accessed | tf_op | source)
XLA Modules:
  0.0 122.3 jit_solution(9802579981276913947)
XLA Ops:
  0.6 0.0 copy-start.4
  0.6 0.0 copy-start.3
  0.7 0.0 copy-start
  0.7 0.8 broadcast_in_dim.4
  1.5 11.0 %all_to_all.30 = bf16[4,128,128]{2,1,0:T(8,128)(2,1)S(1)} all-to-all(bf16[4,128,128]{2,1,0:T(8,128)(2,1)S(1)} %broadcast_in_dim.4), channel_id=1, replica_groups={{0,32,64,96},{1,33,65,97},{2,34,66,98},{3,35,67,99},{4,36,68,100},{5,37..., dimensions={0} | all-to-all | bytes 262144 | tf_op jit(solution)/shard_map/all_to_all | solution.py:48
  12.5 0.1 broadcast_in_dim.5
  12.6 10.7 %all_to_all.31 = bf16[4,4,128,128]{3,2,1,0:T(8,128)(2,1)S(1)} all-to-all(bf16[4,4,128,128]{3,2,1,0:T(8,128)(2,1)S(1)} %broadcast_in_dim.5), channel_id=1, replica_groups={{0,128,256,384},{1,129,257,385},{2,130,258,386},{3,131,259,387},{4,132,..., dimensions={0} | all-to-all | bytes 1048576 | tf_op jit(solution)/shard_map/all_to_all | solution.py:48
  23.4 5.8 %collective-permute-start = (bf16[16,128,128]{2,1,0:T(8,128)(2,1)S(1)}, bf16[16,128,128]{2,1,0:T(8,128)(2,1)S(1)}, u32[]{:S(2)}, u32[]{:S(2)}) collective-permute-start(bf16[16,128,128]{2,1,0:T(8,128)(2,1)S(1)} %bitcast.8), channel_id=1, source_target_pairs={{0,16},{1,17},{2,18},{3,19},{4,20},{5,21},{6,22},{7,23},{8,24},{9,... | collective-permute-start | bytes 1572872 | tf_op jit(solution)/shard_map/ppermute | solution.py:40
  29.1 1.5 %collective-permute-done.other = bf16[16,128,128]{2,1,0:T(8,128)(2,1)S(1)} collective-permute-done((bf16[16,128,128]{2,1,0:T(8,128)(2,1)S(1)}, bf16[16,128,128]{2,1,0:T(8,128)(2,1)S(1)}, u32[]{:S(2)}, u32[]{:S(2)}) %collective-permute-start) | collective-permute-done | bytes 524320 | tf_op jit(solution)/shard_map/ppermute | solution.py:40
  30.6 0.0 copy-done.4
  30.7 0.0 copy-done.3
  30.7 0.0 copy-done
  30.7 0.0 copy-start.1
  30.7 1.0 shard_map.85
  31.7 12.4 %all_to_all.32.parts = bf16[4,4,128,128]{3,2,1,0:T(8,128)(2,1)S(1)} all-to-all(bf16[4,4,128,128]{3,2,1,0:T(8,128)(2,1)S(1)} %get-tuple-element.15), channel_id=1, replica_groups={{0,4,8,12},{1,5,9,13},{2,6,10,14},{3,7,11,15},{16,20,24,28},{17,21,25,2..., dimensions={0} | all-to-all | bytes 1048576 | tf_op jit(solution)/shard_map/all_to_all | solution.py:48
  44.1 0.0 copy-start.2
  44.1 0.0 copy-done.1
  44.1 0.1 shard_map.86
  44.2 30.5 %all-gather = bf16[20,128,128]{2,1,0:T(8,128)(2,1)S(1)} all-gather(bf16[5,128,128]{2,1,0:T(8,128)(2,1)S(1)} %shard_map.86), channel_id=2, replica_groups={{0,1,2,3},{4,5,6,7},{8,9,10,11},{12,13,14,15},{16,17,18,19},{20,21,22,2..., dimensions={0}, use_global_device_ids=true | all-gather | bytes 819200 | tf_op jit(solution)/shard_map/all_gather | solution.py:44
  74.7 0.0 copy-done.2
  74.7 1.0 shard_map.87
  75.6 10.7 %all_to_all.33.parts = bf16[4,6,128,128]{3,2,1,0:T(8,128)(2,1)S(1)} all-to-all(bf16[4,6,128,128]{3,2,1,0:T(8,128)(2,1)S(1)} %get-tuple-element.18), channel_id=1, replica_groups={{0,4,8,12},{1,5,9,13},{2,6,10,14},{3,7,11,15},{16,20,24,28},{17,21,25,2..., dimensions={0} | all-to-all | bytes 1572864 | tf_op jit(solution)/shard_map/all_to_all | solution.py:48
  86.4 1.1 shard_map.88
  87.5 8.7 %collective-permute-start.1 = (bf16[18,128,128]{2,1,0:T(8,128)(2,1)S(1)}, bf16[18,128,128]{2,1,0:T(8,128)(2,1)S(1)}, u32[]{:S(2)}, u32[]{:S(2)}) collective-permute-start(bf16[18,128,128]{2,1,0:T(8,128)(2,1)S(1)} %get-tuple-element.20), channel_id=1, source_target_pairs={{0,16},{1,17},{2,18},{3,19},{4,20},{5,21},{6,22},{7,23},{8,24},{9,... | collective-permute-start | bytes 1769480 | tf_op jit(solution)/shard_map/ppermute | solution.py:40
  96.3 1.6 %collective-permute-done.1.got = bf16[18,128,128]{2,1,0:T(8,128)(2,1)S(1)} collective-permute-done((bf16[18,128,128]{2,1,0:T(8,128)(2,1)S(1)}, bf16[18,128,128]{2,1,0:T(8,128)(2,1)S(1)}, u32[]{:S(2)}, u32[]{:S(2)}) %collective-permute-start.1) | collective-permute-done | bytes 589856 | tf_op jit(solution)/shard_map/ppermute | solution.py:40
  97.9 0.1 shard_map.89
  98.0 13.0 %all_to_all.34.parts = bf16[4,5,128,128]{3,2,1,0:T(8,128)(2,1)S(1)} all-to-all(bf16[4,5,128,128]{3,2,1,0:T(8,128)(2,1)S(1)} %get-tuple-element.21), channel_id=1, replica_groups={{0,128,256,384},{1,129,257,385},{2,130,258,386},{3,131,259,387},{4,132,..., dimensions={0} | all-to-all | bytes 1310720 | tf_op jit(solution)/shard_map/all_to_all | solution.py:48
  111.0 0.1 shard_map.90
  111.2 10.5 %all_to_all.35.parts = bf16[4,2,128,128]{3,2,1,0:T(8,128)(2,1)S(1)} all-to-all(bf16[4,2,128,128]{3,2,1,0:T(8,128)(2,1)S(1)} %get-tuple-element.23), channel_id=1, replica_groups={{0,32,64,96},{1,33,65,97},{2,34,66,98},{3,35,67,99},{4,36,68,100},{5,37..., dimensions={0} | all-to-all | bytes 524288 | tf_op jit(solution)/shard_map/all_to_all | solution.py:48
  121.7 0.7 shard_map.91
Async XLA Ops:
  0.6 30.0 %copy-start.4 = (s32[1,1,16]{2,1,0:T(1,128)S(1)}, s32[1,1,16]{2,1,0:T(1,128)}, u32[]{:S(2)}) copy-start(s32[1,1,16]{2,1,0:T(1,128)} %param.10) | copy-start | bytes 196
  0.6 30.0 %copy-start.3 = (s32[1,1,16]{2,1,0:T(1,128)S(1)}, s32[1,1,16]{2,1,0:T(1,128)}, u32[]{:S(2)}) copy-start(s32[1,1,16]{2,1,0:T(1,128)} %param.9) | copy-start | bytes 196
  0.7 30.0 %copy-start = (bf16[1,1,16,128,128]{4,3,2,1,0:T(8,128)(2,1)S(1)}, bf16[1,1,16,128,128]{4,3,2,1,0:T(8,128)(2,1)}, u32[]{:S(2)}) copy-start(bf16[1,1,16,128,128]{4,3,2,1,0:T(8,128)(2,1)} %param.8) | copy-start | bytes 1572868
  23.4 7.3 %collective-permute-start = (bf16[16,128,128]{2,1,0:T(8,128)(2,1)S(1)}, bf16[16,128,128]{2,1,0:T(8,128)(2,1)S(1)}, u32[]{:S(2)}, u32[]{:S(2)}) collective-permute-start(bf16[16,128,128]{2,1,0:T(8,128)(2,1)S(1)} %bitcast.8), channel_id=1, source_target_pairs={{0,16},{1,17},{2,18},{3,19},{4,20},{5,21},{6,22},{7,23},{8,24},{9,... | collective-permute-start | bytes 1572872 | tf_op jit(solution)/shard_map/ppermute | solution.py:40
  30.7 13.4 %copy-start.1 = (bf16[128,128]{1,0:T(8,128)(2,1)S(1)}, bf16[128,128]{1,0:T(8,128)(2,1)}, u32[]{:S(2)}) copy-start(bf16[128,128]{1,0:T(8,128)(2,1)} %cot.1) | copy-start | bytes 98308
  44.1 30.6 %copy-start.2 = (bf16[128,128]{1,0:T(8,128)(2,1)S(1)}, bf16[128,128]{1,0:T(8,128)(2,1)}, u32[]{:S(2)}) copy-start(bf16[128,128]{1,0:T(8,128)(2,1)} %weight.1) | copy-start | bytes 98308
  87.5 10.4 %collective-permute-start.1 = (bf16[18,128,128]{2,1,0:T(8,128)(2,1)S(1)}, bf16[18,128,128]{2,1,0:T(8,128)(2,1)S(1)}, u32[]{:S(2)}, u32[]{:S(2)}) collective-permute-start(bf16[18,128,128]{2,1,0:T(8,128)(2,1)S(1)} %get-tuple-element.20), channel_id=1, source_target_pairs={{0,16},{1,17},{2,18},{3,19},{4,20},{5,21},{6,22},{7,23},{8,24},{9,... | collective-permute-start | bytes 1769480 | tf_op jit(solution)/shard_map/ppermute | solution.py:40

commit v7 on v6

--- a/solution.py
+++ b/solution.py
@@ -70,6 +70,11 @@
 
 def dot(a, b, dims):
     return lax.dot_general(a, b, (dims, ((), ())), preferred_element_type=F32)
+
+
+def copies(source, out):
+    for k in range(4):
+        out[k] = source[...]
 
 
 def call(body, outs, spaces, scratch=()):
@@ -135,7 +140,7 @@
         out[k, 5] = low
 
 
-def backward_tiles(rows, cols, adj, parts, keep, send, acc):
+def backward_tiles(rows, cols, adj, parts, acc, grad, send):
     core = core_place()
     acc[...] = jnp.zeros_like(acc)
     for t in range(16):
@@ -144,15 +149,15 @@
         d = parts[lax.div(r, 4), lax.rem(r, 4)]
         acc[lax.rem(b, 2), lax.div(b, 2)] += dot(adj[t], d, ((0,), (0,)))
     high, low = split(sum_of(parts, 4) + sum_of(parts, 5))
-    keep[pl.ds(0, 16)] = acc[core]
     send[pl.ds(0, 16)] = acc[1 - core].astype(BF)
-    keep[16] = high.astype(F32) + low.astype(F32)
+    grad[...] = high.astype(F32) + low.astype(F32)
     send[16] = high
     send[17] = low
 
 
-def add_cores(keep, got, out, mine):
-    grad = (keep[16] + (got[16].astype(F32) + got[17].astype(F32))).astype(BF)
+def add_cores(keeps, kept_grad, got, out, mine):
+    keep = keeps.at[core_place()]
+    grad = (kept_grad[...] + (got[16].astype(F32) + got[17].astype(F32))).astype(BF)
     for k in range(4):
         total = keep[pl.ds(4 * k, 4)] + got[pl.ds(4 * k, 4)].astype(F32)
         out[k, pl.ds(0, 4)] = total.astype(BF)
@@ -178,7 +183,8 @@
     own[...] = kept[zl_place()]
 
 
-def add_z(parts, own, out, grad):
+def add_z(parts, own, layer_act, out, grad, act):
+    act[...] = layer_act[...]
     total = own[...]
     for j in range(1, 4):
         total += parts[lax.rem(zl_place() + j, 4), 0].astype(F32)
@@ -192,7 +198,8 @@
     cols = tile_cols.reshape(16)
     tile = (T, F)
 
-    own = exchange(jnp.broadcast_to(features[None], (4, T, F)), "zl")
+    (own,) = call(copies, [((4, T, F), BF)], "v")(features)
+    own = exchange(own, "zl")
     own = exchange(jnp.broadcast_to(own[None], (4, 4, T, F)), "x").reshape(16, T, F)
     other = swap_core(own)
     partial, mine = call(
@@ -208,20 +215,17 @@
         layer, [(tile, F32), ((4, 6, T, F), BF)], "vv", [pltpu.VMEM((4, T, F), F32)]
     )(parts, weight)
     parts = exchange(back, "y")
-    keep, send = call(
-        backward_tiles,
-        [((17, T, F), F32), ((18, T, F), BF)],
-        "ssvv",
-        [pltpu.VMEM((2, 16, T, F), F32)],
+    keeps, grad, send = call(
+        backward_tiles, [((2, 16, T, F), F32), (tile, F32), ((18, T, F), BF)], "ssvv"
     )(rows, cols, adj, parts)
     got = swap_core(send)
-    parts, mine = call(add_cores, [((4, 5, T, F), BF), ((4, T, F), F32)], "vv")(keep, got)
+    parts, mine = call(add_cores, [((4, 5, T, F), BF), ((4, T, F), F32)], "vvv")(keeps, grad, got)
     parts = exchange(parts, "x")
     parts, own = call(
         add_x, [((4, 2, T, F), BF), (tile, F32)], "vv", [pltpu.VMEM((4, T, F), F32)]
     )(parts, mine)
     parts = exchange(parts, "zl")
-    out, grad = call(add_z, [(tile, F32), (tile, F32)], "vv")(parts, own)
+    out, grad, act = call(add_z, [(tile, F32)] * 3, "vvv")(parts, own, act)
     return act, out, grad
 
 

time: 124 us -> 123 us (level)
  no operation moved by 1% of the time
where the time goes in v7:
time: 123 us; the launch traced here: 122 us
  blocking collectives  99.6 us (81%)
  starting transfers between devices  13.6 us (11%)
  Pallas kernels  3.72 us (3%)
  waiting for transfers between devices  3.12 us (3%)
    all_to_all x6, blocking collectives, exchange(): lax.all_to_all(array, BOTH, 0, 0, tiled=True, axis_index_groups=groups(*a...  68.1 us
    all_gather x1, blocking collectives, gather(): lax.all_gather(array, BOTH, axis=0, tiled=False, axis_index_groups=groups...  31.5 us
    ppermute x2, starting transfers between devices, swap_core(): return lax.ppermute(array, BOTH, pairs)  13.6 us
    ppermute x2, waiting for transfers between devices, swap_core(): return lax.ppermute(array, BOTH, pairs)  3.12 us
  transfers between devices with their start and end apart: 2, of which 2 were waited for; matrix products, arithmetic and copies ran while one was open for 0% of the time, Pallas kernels for 0%

profile of v7, /device:TPU:1, one launch (start us, length us, event | category | flops | bytes accessed | tf_op | source)
XLA Modules:
  0.0 121.7 jit_solution(3641449714171811154)
XLA Ops:
  0.6 0.0 copy-start
  0.6 0.0 copy-start.1
  0.7 0.8 copy-done.1
  1.5 0.0 copy-start.4
  1.5 0.0 copy-start.5
  1.5 11.0 %all_to_all.30 = bf16[4,128,128]{2,1,0:T(8,128)(2,1)S(1)} all-to-all(bf16[4,128,128]{2,1,0:T(8,128)(2,1)S(1)} %shard_map.85), channel_id=1, replica_groups={{0,32,64,96},{1,33,65,97},{2,34,66,98},{3,35,67,99},{4,36,68,100},{5,37..., dimensions={0} | all-to-all | bytes 262144 | tf_op jit(solution)/shard_map/all_to_all | solution.py:48
  12.5 0.0 copy-start.2
  12.5 0.1 broadcast_in_dim.2
  12.6 10.7 %all_to_all.31 = bf16[4,4,128,128]{3,2,1,0:T(8,128)(2,1)S(1)} all-to-all(bf16[4,4,128,128]{3,2,1,0:T(8,128)(2,1)S(1)} %broadcast_in_dim.2), channel_id=1, replica_groups={{0,128,256,384},{1,129,257,385},{2,130,258,386},{3,131,259,387},{4,132,..., dimensions={0} | all-to-all | bytes 1048576 | tf_op jit(solution)/shard_map/all_to_all | solution.py:48
  23.3 5.8 %collective-permute-start = (bf16[16,128,128]{2,1,0:T(8,128)(2,1)S(1)}, bf16[16,128,128]{2,1,0:T(8,128)(2,1)S(1)}, u32[]{:S(2)}, u32[]{:S(2)}) collective-permute-start(bf16[16,128,128]{2,1,0:T(8,128)(2,1)S(1)} %bitcast.8), channel_id=1, source_target_pairs={{0,16},{1,17},{2,18},{3,19},{4,20},{5,21},{6,22},{7,23},{8,24},{9,... | collective-permute-start | bytes 1572872 | tf_op jit(solution)/shard_map/ppermute | solution.py:40
  29.1 1.5 %collective-permute-done.other = bf16[16,128,128]{2,1,0:T(8,128)(2,1)S(1)} collective-permute-done((bf16[16,128,128]{2,1,0:T(8,128)(2,1)S(1)}, bf16[16,128,128]{2,1,0:T(8,128)(2,1)S(1)}, u32[]{:S(2)}, u32[]{:S(2)}) %collective-permute-start) | collective-permute-done | bytes 524320 | tf_op jit(solution)/shard_map/ppermute | solution.py:40
  30.6 0.0 copy-done
  30.6 0.0 copy-done.4
  30.6 0.0 copy-done.5
  30.6 0.0 copy-start.3
  30.7 1.0 shard_map.86
  31.7 12.4 %all_to_all.32.parts = bf16[4,4,128,128]{3,2,1,0:T(8,128)(2,1)S(1)} all-to-all(bf16[4,4,128,128]{3,2,1,0:T(8,128)(2,1)S(1)} %get-tuple-element.17), channel_id=1, replica_groups={{0,4,8,12},{1,5,9,13},{2,6,10,14},{3,7,11,15},{16,20,24,28},{17,21,25,2..., dimensions={0} | all-to-all | bytes 1048576 | tf_op jit(solution)/shard_map/all_to_all | solution.py:48
  44.1 0.0 copy-done.2
  44.1 0.1 shard_map.87
  44.2 31.5 %all-gather = bf16[20,128,128]{2,1,0:T(8,128)(2,1)S(1)} all-gather(bf16[5,128,128]{2,1,0:T(8,128)(2,1)S(1)} %shard_map.87), channel_id=2, replica_groups={{0,1,2,3},{4,5,6,7},{8,9,10,11},{12,13,14,15},{16,17,18,19},{20,21,22,2..., dimensions={0}, use_global_device_ids=true | all-gather | bytes 819200 | tf_op jit(solution)/shard_map/all_gather | solution.py:44
  75.6 0.0 copy-done.3
  75.6 0.6 shard_map.88
  76.3 10.7 %all_to_all.33.parts = bf16[4,6,128,128]{3,2,1,0:T(8,128)(2,1)S(1)} all-to-all(bf16[4,6,128,128]{3,2,1,0:T(8,128)(2,1)S(1)} %get-tuple-element.19), channel_id=1, replica_groups={{0,4,8,12},{1,5,9,13},{2,6,10,14},{3,7,11,15},{16,20,24,28},{17,21,25,2..., dimensions={0} | all-to-all | bytes 1572864 | tf_op jit(solution)/shard_map/all_to_all | solution.py:48
  87.0 1.0 shard_map.89
  88.1 7.8 %collective-permute-start.1 = (bf16[18,128,128]{2,1,0:T(8,128)(2,1)S(1)}, bf16[18,128,128]{2,1,0:T(8,128)(2,1)S(1)}, u32[]{:S(2)}, u32[]{:S(2)}) collective-permute-start(bf16[18,128,128]{2,1,0:T(8,128)(2,1)S(1)} %get-tuple-element.22), channel_id=1, source_target_pairs={{0,16},{1,17},{2,18},{3,19},{4,20},{5,21},{6,22},{7,23},{8,24},{9,... | collective-permute-start | bytes 1769480 | tf_op jit(solution)/shard_map/ppermute | solution.py:40
  95.9 1.6 %collective-permute-done.1.got = bf16[18,128,128]{2,1,0:T(8,128)(2,1)S(1)} collective-permute-done((bf16[18,128,128]{2,1,0:T(8,128)(2,1)S(1)}, bf16[18,128,128]{2,1,0:T(8,128)(2,1)S(1)}, u32[]{:S(2)}, u32[]{:S(2)}) %collective-permute-start.1) | collective-permute-done | bytes 589856 | tf_op jit(solution)/shard_map/ppermute | solution.py:40
  97.5 0.1 shard_map.90
  97.7 13.0 %all_to_all.34.parts = bf16[4,5,128,128]{3,2,1,0:T(8,128)(2,1)S(1)} all-to-all(bf16[4,5,128,128]{3,2,1,0:T(8,128)(2,1)S(1)} %get-tuple-element.23), channel_id=1, replica_groups={{0,128,256,384},{1,129,257,385},{2,130,258,386},{3,131,259,387},{4,132,..., dimensions={0} | all-to-all | bytes 1310720 | tf_op jit(solution)/shard_map/all_to_all | solution.py:48
  110.7 0.1 shard_map.91
  110.8 10.2 %all_to_all.35.parts = bf16[4,2,128,128]{3,2,1,0:T(8,128)(2,1)S(1)} all-to-all(bf16[4,2,128,128]{3,2,1,0:T(8,128)(2,1)S(1)} %get-tuple-element.25), channel_id=1, replica_groups={{0,32,64,96},{1,33,65,97},{2,34,66,98},{3,35,67,99},{4,36,68,100},{5,37..., dimensions={0} | all-to-all | bytes 524288 | tf_op jit(solution)/shard_map/all_to_all | solution.py:48
  121.0 0.7 shard_map.92
  (1 shorter events, 0.0 us)
Async XLA Ops:
  0.6 30.0 %copy-start = (bf16[1,1,16,128,128]{4,3,2,1,0:T(8,128)(2,1)S(1)}, bf16[1,1,16,128,128]{4,3,2,1,0:T(8,128)(2,1)}, u32[]{:S(2)}) copy-start(bf16[1,1,16,128,128]{4,3,2,1,0:T(8,128)(2,1)} %param.8) | copy-start | bytes 1572868
  0.6 0.8 copy-start.1
  1.5 29.2 %copy-start.4 = (s32[1,1,16]{2,1,0:T(1,128)S(1)}, s32[1,1,16]{2,1,0:T(1,128)}, u32[]{:S(2)}) copy-start(s32[1,1,16]{2,1,0:T(1,128)} %param.9) | copy-start | bytes 196
  1.5 29.2 %copy-start.5 = (s32[1,1,16]{2,1,0:T(1,128)S(1)}, s32[1,1,16]{2,1,0:T(1,128)}, u32[]{:S(2)}) copy-start(s32[1,1,16]{2,1,0:T(1,128)} %param.10) | copy-start | bytes 196
  12.5 31.6 %copy-start.2 = (bf16[128,128]{1,0:T(8,128)(2,1)S(1)}, bf16[128,128]{1,0:T(8,128)(2,1)}, u32[]{:S(2)}) copy-start(bf16[128,128]{1,0:T(8,128)(2,1)} %cot.1) | copy-start | bytes 98308
  23.3 7.3 %collective-permute-start = (bf16[16,128,128]{2,1,0:T(8,128)(2,1)S(1)}, bf16[16,128,128]{2,1,0:T(8,128)(2,1)S(1)}, u32[]{:S(2)}, u32[]{:S(2)}) collective-permute-start(bf16[16,128,128]{2,1,0:T(8,128)(2,1)S(1)} %bitcast.8), channel_id=1, source_target_pairs={{0,16},{1,17},{2,18},{3,19},{4,20},{5,21},{6,22},{7,23},{8,24},{9,... | collective-permute-start | bytes 1572872 | tf_op jit(solution)/shard_map/ppermute | solution.py:40
  30.6 45.0 %copy-start.3 = (bf16[128,128]{1,0:T(8,128)(2,1)S(1)}, bf16[128,128]{1,0:T(8,128)(2,1)}, u32[]{:S(2)}) copy-start(bf16[128,128]{1,0:T(8,128)(2,1)} %weight.1) | copy-start | bytes 98308
  88.1 9.4 %collective-permute-start.1 = (bf16[18,128,128]{2,1,0:T(8,128)(2,1)S(1)}, bf16[18,128,128]{2,1,0:T(8,128)(2,1)S(1)}, u32[]{:S(2)}, u32[]{:S(2)}) collective-permute-start(bf16[18,128,128]{2,1,0:T(8,128)(2,1)S(1)} %get-tuple-element.22), channel_id=1, source_target_pairs={{0,16},{1,17},{2,18},{3,19},{4,20},{5,21},{6,22},{7,23},{8,24},{9,... | collective-permute-start | bytes 1769480 | tf_op jit(solution)/shard_map/ppermute | solution.py:40

commit v8 on v7

--- a/solution.py
+++ b/solution.py
@@ -100,14 +100,15 @@
     return own
 
 
-def forward_tiles(rows, cols, adj, own, other, out, mine, acc):
+def forward_tiles(rows, cols, adj, own, other, out, mine, acc, products):
     acc[...] = jnp.zeros_like(acc)
     for t in range(16):
         b = cols[t]
         spot = lax.div(b, 2)
         x = jnp.where(lax.rem(b, 2) == core_place(), own[spot], other[spot])
-        r = rows[t]
-        acc[r] += dot(adj[t], x, ((1,), (0,)))
+        products[t] = dot(adj[t], x, ((1,), (0,)))
+    for t in range(16):
+        acc[rows[t]] += products[t]
     out[...] = acc[...].astype(BF).reshape(4, 4, T, F)
     mine[...] = acc[pl.ds(y_place() * 4, 4)]
 
@@ -140,14 +141,16 @@
         out[k, 5] = low
 
 
-def backward_tiles(rows, cols, adj, parts, acc, grad, send):
+def backward_tiles(rows, cols, adj, parts, acc, grad, send, products):
     core = core_place()
     acc[...] = jnp.zeros_like(acc)
     for t in range(16):
         r = rows[t]
+        d = parts[lax.div(r, 4), lax.rem(r, 4)]
+        products[t] = dot(adj[t], d, ((0,), (0,)))
+    for t in range(16):
         b = cols[t]
-        d = parts[lax.div(r, 4), lax.rem(r, 4)]
-        acc[lax.rem(b, 2), lax.div(b, 2)] += dot(adj[t], d, ((0,), (0,)))
+        acc[lax.rem(b, 2), lax.div(b, 2)] += products[t]
     high, low = split(sum_of(parts, 4) + sum_of(parts, 5))
     send[pl.ds(0, 16)] = acc[1 - core].astype(BF)
     grad[...] = high.astype(F32) + low.astype(F32)
@@ -206,7 +209,7 @@
         forward_tiles,
         [((4, 4, T, F), BF), ((4, T, F), F32)],
         "ssvvv",
-        [pltpu.VMEM((16, T, F), F32)],
+        [pltpu.VMEM((16, T, F), F32)] * 2,
     )(rows, cols, adj, own, other)
     parts = exchange(partial, "y")
     (summed,) = call(add_y, [((5, T, F), BF)], "vvv")(parts, mine, cotangent)
@@ -216,7 +219,10 @@
     )(parts, weight)
     parts = exchange(back, "y")
     keeps, grad, send = call(
-        backward_tiles, [((2, 16, T, F), F32), (tile, F32), ((18, T, F), BF)], "ssvv"
+        backward_tiles,
+        [((2, 16, T, F), F32), (tile, F32), ((18, T, F), BF)],
+        "ssvv",
+        [pltpu.VMEM((16, T, F), F32)],
     )(rows, cols, adj, parts)
     got = swap_core(send)
     parts, mine = call(add_cores, [((4, 5, T, F), BF), ((4, T, F), F32)], "vvv")(keeps, grad, got)

time: 123 us -> 123 us (level)
  no operation moved by 1% of the time
where the time goes in v8:
time: 123 us; the launch traced here: 121 us
  blocking collectives  99.4 us (81%)
  starting transfers between devices  13.5 us (11%)
  Pallas kernels  3.71 us (3%)
  waiting for transfers between devices  3.12 us (3%)
    all_to_all x6, blocking collectives, exchange(): lax.all_to_all(array, BOTH, 0, 0, tiled=True, axis_index_groups=groups(*a...  68 us
    all_gather x1, blocking collectives, gather(): lax.all_gather(array, BOTH, axis=0, tiled=False, axis_index_groups=groups...  31.5 us
    ppermute x2, starting transfers between devices, swap_core(): return lax.ppermute(array, BOTH, pairs)  13.5 us
    ppermute x2, waiting for transfers between devices, swap_core(): return lax.ppermute(array, BOTH, pairs)  3.12 us
  transfers between devices with their start and end apart: 2, of which 2 were waited for; matrix products, arithmetic and copies ran while one was open for 0% of the time, Pallas kernels for 0%

profile of v8, /device:TPU:1, one launch (start us, length us, event | category | flops | bytes accessed | tf_op | source)
XLA Modules:
  0.0 121.4 jit_solution(4711823007676433932)
XLA Ops:
  0.6 0.0 copy-start
  0.6 0.0 copy-start.1
  0.7 0.8 copy-done.1
  1.5 0.0 copy-start.4
  1.5 0.0 copy-start.5
  1.5 11.0 %all_to_all.30 = bf16[4,128,128]{2,1,0:T(8,128)(2,1)S(1)} all-to-all(bf16[4,128,128]{2,1,0:T(8,128)(2,1)S(1)} %shard_map.85), channel_id=1, replica_groups={{0,32,64,96},{1,33,65,97},{2,34,66,98},{3,35,67,99},{4,36,68,100},{5,37..., dimensions={0} | all-to-all | bytes 262144 | tf_op jit(solution)/shard_map/all_to_all | solution.py:48
  12.5 0.0 copy-start.2
  12.5 0.1 broadcast_in_dim.2
  12.6 10.7 %all_to_all.31 = bf16[4,4,128,128]{3,2,1,0:T(8,128)(2,1)S(1)} all-to-all(bf16[4,4,128,128]{3,2,1,0:T(8,128)(2,1)S(1)} %broadcast_in_dim.2), channel_id=1, replica_groups={{0,128,256,384},{1,129,257,385},{2,130,258,386},{3,131,259,387},{4,132,..., dimensions={0} | all-to-all | bytes 1048576 | tf_op jit(solution)/shard_map/all_to_all | solution.py:48
  23.3 5.8 %collective-permute-start = (bf16[16,128,128]{2,1,0:T(8,128)(2,1)S(1)}, bf16[16,128,128]{2,1,0:T(8,128)(2,1)S(1)}, u32[]{:S(2)}, u32[]{:S(2)}) collective-permute-start(bf16[16,128,128]{2,1,0:T(8,128)(2,1)S(1)} %bitcast.8), channel_id=1, source_target_pairs={{0,16},{1,17},{2,18},{3,19},{4,20},{5,21},{6,22},{7,23},{8,24},{9,... | collective-permute-start | bytes 1572872 | tf_op jit(solution)/shard_map/ppermute | solution.py:40
  29.1 1.5 %collective-permute-done.other = bf16[16,128,128]{2,1,0:T(8,128)(2,1)S(1)} collective-permute-done((bf16[16,128,128]{2,1,0:T(8,128)(2,1)S(1)}, bf16[16,128,128]{2,1,0:T(8,128)(2,1)S(1)}, u32[]{:S(2)}, u32[]{:S(2)}) %collective-permute-start) | collective-permute-done | bytes 524320 | tf_op jit(solution)/shard_map/ppermute | solution.py:40
  30.6 0.0 copy-done
  30.6 0.0 copy-done.4
  30.6 0.0 copy-done.5
  30.6 0.0 copy-start.3
  30.7 1.0 shard_map.86
  31.7 12.4 %all_to_all.32.parts = bf16[4,4,128,128]{3,2,1,0:T(8,128)(2,1)S(1)} all-to-all(bf16[4,4,128,128]{3,2,1,0:T(8,128)(2,1)S(1)} %get-tuple-element.17), channel_id=1, replica_groups={{0,4,8,12},{1,5,9,13},{2,6,10,14},{3,7,11,15},{16,20,24,28},{17,21,25,2..., dimensions={0} | all-to-all | bytes 1048576 | tf_op jit(solution)/shard_map/all_to_all | solution.py:48
  44.1 0.0 copy-done.2
  44.1 0.1 shard_map.87
  44.2 31.5 %all-gather = bf16[20,128,128]{2,1,0:T(8,128)(2,1)S(1)} all-gather(bf16[5,128,128]{2,1,0:T(8,128)(2,1)S(1)} %shard_map.87), channel_id=2, replica_groups={{0,1,2,3},{4,5,6,7},{8,9,10,11},{12,13,14,15},{16,17,18,19},{20,21,22,2..., dimensions={0}, use_global_device_ids=true | all-gather | bytes 819200 | tf_op jit(solution)/shard_map/all_gather | solution.py:44
  75.6 0.0 copy-done.3
  75.6 0.6 shard_map.88
  76.2 10.7 %all_to_all.33.parts = bf16[4,6,128,128]{3,2,1,0:T(8,128)(2,1)S(1)} all-to-all(bf16[4,6,128,128]{3,2,1,0:T(8,128)(2,1)S(1)} %get-tuple-element.19), channel_id=1, replica_groups={{0,4,8,12},{1,5,9,13},{2,6,10,14},{3,7,11,15},{16,20,24,28},{17,21,25,2..., dimensions={0} | all-to-all | bytes 1572864 | tf_op jit(solution)/shard_map/all_to_all | solution.py:48
  87.0 1.0 shard_map.89
  88.0 7.8 %collective-permute-start.1 = (bf16[18,128,128]{2,1,0:T(8,128)(2,1)S(1)}, bf16[18,128,128]{2,1,0:T(8,128)(2,1)S(1)}, u32[]{:S(2)}, u32[]{:S(2)}) collective-permute-start(bf16[18,128,128]{2,1,0:T(8,128)(2,1)S(1)} %get-tuple-element.22), channel_id=1, source_target_pairs={{0,16},{1,17},{2,18},{3,19},{4,20},{5,21},{6,22},{7,23},{8,24},{9,... | collective-permute-start | bytes 1769480 | tf_op jit(solution)/shard_map/ppermute | solution.py:40
  95.8 1.6 %collective-permute-done.1.got = bf16[18,128,128]{2,1,0:T(8,128)(2,1)S(1)} collective-permute-done((bf16[18,128,128]{2,1,0:T(8,128)(2,1)S(1)}, bf16[18,128,128]{2,1,0:T(8,128)(2,1)S(1)}, u32[]{:S(2)}, u32[]{:S(2)}) %collective-permute-start.1) | collective-permute-done | bytes 589856 | tf_op jit(solution)/shard_map/ppermute | solution.py:40
  97.4 0.1 shard_map.90
  97.6 13.0 %all_to_all.34.parts = bf16[4,5,128,128]{3,2,1,0:T(8,128)(2,1)S(1)} all-to-all(bf16[4,5,128,128]{3,2,1,0:T(8,128)(2,1)S(1)} %get-tuple-element.23), channel_id=1, replica_groups={{0,128,256,384},{1,129,257,385},{2,130,258,386},{3,131,259,387},{4,132,..., dimensions={0} | all-to-all | bytes 1310720 | tf_op jit(solution)/shard_map/all_to_all | solution.py:48
  110.6 0.1 shard_map.91
  110.7 10.0 %all_to_all.35.parts = bf16[4,2,128,128]{3,2,1,0:T(8,128)(2,1)S(1)} all-to-all(bf16[4,2,128,128]{3,2,1,0:T(8,128)(2,1)S(1)} %get-tuple-element.25), channel_id=1, replica_groups={{0,32,64,96},{1,33,65,97},{2,34,66,98},{3,35,67,99},{4,36,68,100},{5,37..., dimensions={0} | all-to-all | bytes 524288 | tf_op jit(solution)/shard_map/all_to_all | solution.py:48
  120.7 0.7 shard_map.92
  (1 shorter events, 0.0 us)
Async XLA Ops:
  0.6 30.0 %copy-start = (bf16[1,1,16,128,128]{4,3,2,1,0:T(8,128)(2,1)S(1)}, bf16[1,1,16,128,128]{4,3,2,1,0:T(8,128)(2,1)}, u32[]{:S(2)}) copy-start(bf16[1,1,16,128,128]{4,3,2,1,0:T(8,128)(2,1)} %param.8) | copy-start | bytes 1572868
  0.6 0.8 copy-start.1
  1.5 29.2 %copy-start.4 = (s32[1,1,16]{2,1,0:T(1,128)S(1)}, s32[1,1,16]{2,1,0:T(1,128)}, u32[]{:S(2)}) copy-start(s32[1,1,16]{2,1,0:T(1,128)} %param.9) | copy-start | bytes 196
  1.5 29.2 %copy-start.5 = (s32[1,1,16]{2,1,0:T(1,128)S(1)}, s32[1,1,16]{2,1,0:T(1,128)}, u32[]{:S(2)}) copy-start(s32[1,1,16]{2,1,0:T(1,128)} %param.10) | copy-start | bytes 196
  12.5 31.6 %copy-start.2 = (bf16[128,128]{1,0:T(8,128)(2,1)S(1)}, bf16[128,128]{1,0:T(8,128)(2,1)}, u32[]{:S(2)}) copy-start(bf16[128,128]{1,0:T(8,128)(2,1)} %cot.1) | copy-start | bytes 98308
  23.3 7.3 %collective-permute-start = (bf16[16,128,128]{2,1,0:T(8,128)(2,1)S(1)}, bf16[16,128,128]{2,1,0:T(8,128)(2,1)S(1)}, u32[]{:S(2)}, u32[]{:S(2)}) collective-permute-start(bf16[16,128,128]{2,1,0:T(8,128)(2,1)S(1)} %bitcast.8), channel_id=1, source_target_pairs={{0,16},{1,17},{2,18},{3,19},{4,20},{5,21},{6,22},{7,23},{8,24},{9,... | collective-permute-start | bytes 1572872 | tf_op jit(solution)/shard_map/ppermute | solution.py:40
  30.6 45.0 %copy-start.3 = (bf16[128,128]{1,0:T(8,128)(2,1)S(1)}, bf16[128,128]{1,0:T(8,128)(2,1)}, u32[]{:S(2)}) copy-start(bf16[128,128]{1,0:T(8,128)(2,1)} %weight.1) | copy-start | bytes 98308
  88.0 9.4 %collective-permute-start.1 = (bf16[18,128,128]{2,1,0:T(8,128)(2,1)S(1)}, bf16[18,128,128]{2,1,0:T(8,128)(2,1)S(1)}, u32[]{:S(2)}, u32[]{:S(2)}) collective-permute-start(bf16[18,128,128]{2,1,0:T(8,128)(2,1)S(1)} %get-tuple-element.22), channel_id=1, source_target_pairs={{0,16},{1,17},{2,18},{3,19},{4,20},{5,21},{6,22},{7,23},{8,24},{9,... | collective-permute-start | bytes 1769480 | tf_op jit(solution)/shard_map/ppermute | solution.py:40

commit v9 on v7

--- a/solution.py
+++ b/solution.py
@@ -27,12 +27,15 @@
         yield dict(zip(SIZES, values))
 
 
-def groups(*axes):
+def groups(axis, turned=False):
     found = {}
     for place in places():
-        key = tuple(v for n, v in place.items() if n not in axes)
-        found.setdefault(key, []).append(position(place))
-    return list(found.values())
+        key = tuple(v for n, v in place.items() if n != axis)
+        found.setdefault(key, []).append(place)
+    return [
+        [position(p) for p in (g[::-1] if turned and g[0]["core"] else g)]
+        for g in found.values()
+    ]
 
 
 def swap_core(array):
@@ -44,8 +47,9 @@
     return lax.all_gather(array, BOTH, axis=0, tiled=False, axis_index_groups=groups(axis))
 
 
-def exchange(array, *axes):
-    return lax.all_to_all(array, BOTH, 0, 0, tiled=True, axis_index_groups=groups(*axes))
+def exchange(array, axis, turned=False):
+    members = groups(axis, turned)
+    return lax.all_to_all(array, BOTH, 0, 0, tiled=True, axis_index_groups=members)
 
 
 def core_place():
@@ -92,6 +96,10 @@
 def split(grad):
     high = grad.astype(BF)
     return high, (grad - high.astype(F32)).astype(BF)
+
+
+def slot(place):
+    return place + core_place() * (3 - 2 * place)
 
 
 def plus_others(own, parts, place, count):
@@ -160,24 +168,22 @@
     grad = (kept_grad[...] + (got[16].astype(F32) + got[17].astype(F32))).astype(BF)
     for k in range(4):
         total = keep[pl.ds(4 * k, 4)] + got[pl.ds(4 * k, 4)].astype(F32)
-        out[k, pl.ds(0, 4)] = total.astype(BF)
+        out[slot(k), pl.ds(0, 4)] = total.astype(BF)
         out[k, 4] = grad
     start = x_place() * 4
     mine[...] = keep[pl.ds(start, 4)] + got[pl.ds(start, 4)].astype(F32)
 
 
 def sum_of(parts, spot):
-    total = parts[0, spot].astype(F32)
-    for k in range(1, 4):
-        total += parts[k, spot].astype(F32)
-    return total
+    one, two, three, four = (parts[k, spot].astype(F32) for k in range(4))
+    return (one + four) + (two + three)
 
 
 def add_x(parts, mine, out, own, kept):
-    total = plus_others(mine[...], parts, x_place(), 4)
+    total = plus_others(mine[...], parts, slot(x_place()), 4)
     grad = sum_of(parts, 4).astype(BF)
     for k in range(4):
-        out[k, 0] = total[k].astype(BF)
+        out[slot(k), 0] = total[k].astype(BF)
         out[k, 1] = grad
     kept[...] = total
     own[...] = kept[zl_place()]
@@ -187,7 +193,7 @@
     act[...] = layer_act[...]
     total = own[...]
     for j in range(1, 4):
-        total += parts[lax.rem(zl_place() + j, 4), 0].astype(F32)
+        total += parts[lax.rem(slot(zl_place()) + j, 4), 0].astype(F32)
     out[...] = total
     grad[...] = sum_of(parts, 1)
 
@@ -220,11 +226,11 @@
     )(rows, cols, adj, parts)
     got = swap_core(send)
     parts, mine = call(add_cores, [((4, 5, T, F), BF), ((4, T, F), F32)], "vvv")(keeps, grad, got)
-    parts = exchange(parts, "x")
+    parts = exchange(parts, "x", True)
     parts, own = call(
         add_x, [((4, 2, T, F), BF), (tile, F32)], "vv", [pltpu.VMEM((4, T, F), F32)]
     )(parts, mine)
-    parts = exchange(parts, "zl")
+    parts = exchange(parts, "zl", True)
     out, grad, act = call(add_z, [(tile, F32)] * 3, "vvv")(parts, own, act)
     return act, out, grad
 

time: 123 us -> 123 us (level)
  the two profiles are of different devices: /device:TPU:1 before, /device:TPU:6 now
where the time goes in v9:
time: 123 us; the launch traced here: 122 us
  blocking collectives  109 us (89%)
  waiting for transfers between devices  3.85 us (3%)
  starting transfers between devices  3.83 us (3%)
  Pallas kernels  3.74 us (3%)
    all_to_all x6, blocking collectives, exchange(): lax.all_to_all(array, BOTH, 0, 0, tiled=True, axis_index_groups=members)  74.6 us
    all_gather x1, blocking collectives, gather(): lax.all_gather(array, BOTH, axis=0, tiled=False, axis_index_groups=groups...  34.5 us
    ppermute x2, waiting for transfers between devices, swap_core(): return lax.ppermute(array, BOTH, pairs)  3.85 us
    ppermute x2, starting transfers between devices, swap_core(): return lax.ppermute(array, BOTH, pairs)  3.83 us
  transfers between devices with their start and end apart: 2, of which 2 were waited for; matrix products, arithmetic and copies ran while one was open for 0% of the time, Pallas kernels for 0%

profile of v9, /device:TPU:6, one launch (start us, length us, event | category | flops | bytes accessed | tf_op | source)
XLA Modules:
  0.0 122.2 jit_solution(8376646809688673484)
XLA Ops:
  0.6 0.0 copy-start
  0.6 0.0 copy-start.1
  0.7 0.8 copy-done.1
  1.5 0.0 copy-start.4
  1.5 0.0 copy-start.5
  1.5 11.8 %all_to_all.30 = bf16[4,128,128]{2,1,0:T(8,128)(2,1)S(1)} all-to-all(bf16[4,128,128]{2,1,0:T(8,128)(2,1)S(1)} %shard_map.85), channel_id=1, replica_groups={{0,32,64,96},{1,33,65,97},{2,34,66,98},{3,35,67,99},{4,36,68,100},{5,37..., dimensions={0} | all-to-all | bytes 262144 | tf_op jit(solution)/shard_map/all_to_all | solution.py:52
  13.3 0.0 copy-start.2
  13.3 0.1 broadcast_in_dim.2
  13.4 10.8 %all_to_all.31 = bf16[4,4,128,128]{3,2,1,0:T(8,128)(2,1)S(1)} all-to-all(bf16[4,4,128,128]{3,2,1,0:T(8,128)(2,1)S(1)} %broadcast_in_dim.2), channel_id=1, replica_groups={{0,128,256,384},{1,129,257,385},{2,130,258,386},{3,131,259,387},{4,132,..., dimensions={0} | all-to-all | bytes 1048576 | tf_op jit(solution)/shard_map/all_to_all | solution.py:52
  24.1 1.9 %collective-permute-start = (bf16[16,128,128]{2,1,0:T(8,128)(2,1)S(1)}, bf16[16,128,128]{2,1,0:T(8,128)(2,1)S(1)}, u32[]{:S(2)}, u32[]{:S(2)}) collective-permute-start(bf16[16,128,128]{2,1,0:T(8,128)(2,1)S(1)} %bitcast.8), channel_id=1, source_target_pairs={{0,16},{1,17},{2,18},{3,19},{4,20},{5,21},{6,22},{7,23},{8,24},{9,... | collective-permute-start | bytes 1572872 | tf_op jit(solution)/shard_map/ppermute | solution.py:43
  26.0 1.9 %collective-permute-done.other = bf16[16,128,128]{2,1,0:T(8,128)(2,1)S(1)} collective-permute-done((bf16[16,128,128]{2,1,0:T(8,128)(2,1)S(1)}, bf16[16,128,128]{2,1,0:T(8,128)(2,1)S(1)}, u32[]{:S(2)}, u32[]{:S(2)}) %collective-permute-start) | collective-permute-done | bytes 524320 | tf_op jit(solution)/shard_map/ppermute | solution.py:43
  27.9 0.0 copy-done
  27.9 0.0 copy-done.4
  27.9 0.0 copy-done.5
  27.9 0.0 copy-start.3
  27.9 1.0 shard_map.86
  29.0 13.8 %all_to_all.32.parts = bf16[4,4,128,128]{3,2,1,0:T(8,128)(2,1)S(1)} all-to-all(bf16[4,4,128,128]{3,2,1,0:T(8,128)(2,1)S(1)} %get-tuple-element.17), channel_id=1, replica_groups={{0,4,8,12},{1,5,9,13},{2,6,10,14},{3,7,11,15},{16,20,24,28},{17,21,25,2..., dimensions={0} | all-to-all | bytes 1048576 | tf_op jit(solution)/shard_map/all_to_all | solution.py:52
  42.8 0.0 copy-done.2
  42.8 0.1 shard_map.87
  42.9 34.5 %all-gather = bf16[20,128,128]{2,1,0:T(8,128)(2,1)S(1)} all-gather(bf16[5,128,128]{2,1,0:T(8,128)(2,1)S(1)} %shard_map.87), channel_id=2, replica_groups={{0,1,2,3},{4,5,6,7},{8,9,10,11},{12,13,14,15},{16,17,18,19},{20,21,22,2..., dimensions={0}, use_global_device_ids=true | all-gather | bytes 819200 | tf_op jit(solution)/shard_map/all_gather | solution.py:47
  77.4 0.0 copy-done.3
  77.4 0.6 shard_map.88
  78.0 11.9 %all_to_all.33.parts = bf16[4,6,128,128]{3,2,1,0:T(8,128)(2,1)S(1)} all-to-all(bf16[4,6,128,128]{3,2,1,0:T(8,128)(2,1)S(1)} %get-tuple-element.19), channel_id=1, replica_groups={{0,4,8,12},{1,5,9,13},{2,6,10,14},{3,7,11,15},{16,20,24,28},{17,21,25,2..., dimensions={0} | all-to-all | bytes 1572864 | tf_op jit(solution)/shard_map/all_to_all | solution.py:52
  89.9 1.1 shard_map.89
  91.0 1.9 %collective-permute-start.1 = (bf16[18,128,128]{2,1,0:T(8,128)(2,1)S(1)}, bf16[18,128,128]{2,1,0:T(8,128)(2,1)S(1)}, u32[]{:S(2)}, u32[]{:S(2)}) collective-permute-start(bf16[18,128,128]{2,1,0:T(8,128)(2,1)S(1)} %get-tuple-element.22), channel_id=1, source_target_pairs={{0,16},{1,17},{2,18},{3,19},{4,20},{5,21},{6,22},{7,23},{8,24},{9,... | collective-permute-start | bytes 1769480 | tf_op jit(solution)/shard_map/ppermute | solution.py:43
  92.9 2.0 %collective-permute-done.1.got = bf16[18,128,128]{2,1,0:T(8,128)(2,1)S(1)} collective-permute-done((bf16[18,128,128]{2,1,0:T(8,128)(2,1)S(1)}, bf16[18,128,128]{2,1,0:T(8,128)(2,1)S(1)}, u32[]{:S(2)}, u32[]{:S(2)}) %collective-permute-start.1) | collective-permute-done | bytes 589856 | tf_op jit(solution)/shard_map/ppermute | solution.py:43
  94.9 0.2 shard_map.90
  95.0 14.4 %all_to_all.34.parts = bf16[4,5,128,128]{3,2,1,0:T(8,128)(2,1)S(1)} all-to-all(bf16[4,5,128,128]{3,2,1,0:T(8,128)(2,1)S(1)} %get-tuple-element.23), channel_id=1, replica_groups={{0,128,256,384},{1,129,257,385},{2,130,258,386},{3,131,259,387},{4,132,..., dimensions={0} | all-to-all | bytes 1310720 | tf_op jit(solution)/shard_map/all_to_all | solution.py:52
  109.5 0.1 shard_map.91
  109.6 11.9 %all_to_all.35.parts = bf16[4,2,128,128]{3,2,1,0:T(8,128)(2,1)S(1)} all-to-all(bf16[4,2,128,128]{3,2,1,0:T(8,128)(2,1)S(1)} %get-tuple-element.25), channel_id=1, replica_groups={{0,32,64,96},{1,33,65,97},{2,34,66,98},{3,35,67,99},{4,36,68,100},{5,37..., dimensions={0} | all-to-all | bytes 524288 | tf_op jit(solution)/shard_map/all_to_all | solution.py:52
  121.5 0.7 shard_map.92
  (1 shorter events, 0.0 us)
Async XLA Ops:
  0.6 27.3 %copy-start = (bf16[1,1,16,128,128]{4,3,2,1,0:T(8,128)(2,1)S(1)}, bf16[1,1,16,128,128]{4,3,2,1,0:T(8,128)(2,1)}, u32[]{:S(2)}) copy-start(bf16[1,1,16,128,128]{4,3,2,1,0:T(8,128)(2,1)} %param.8) | copy-start | bytes 1572868
  0.6 0.8 copy-start.1
  1.5 26.5 %copy-start.4 = (s32[1,1,16]{2,1,0:T(1,128)S(1)}, s32[1,1,16]{2,1,0:T(1,128)}, u32[]{:S(2)}) copy-start(s32[1,1,16]{2,1,0:T(1,128)} %param.9) | copy-start | bytes 196
  1.5 26.5 %copy-start.5 = (s32[1,1,16]{2,1,0:T(1,128)S(1)}, s32[1,1,16]{2,1,0:T(1,128)}, u32[]{:S(2)}) copy-start(s32[1,1,16]{2,1,0:T(1,128)} %param.10) | copy-start | bytes 196
  13.3 29.6 %copy-start.2 = (bf16[128,128]{1,0:T(8,128)(2,1)S(1)}, bf16[128,128]{1,0:T(8,128)(2,1)}, u32[]{:S(2)}) copy-start(bf16[128,128]{1,0:T(8,128)(2,1)} %cot.1) | copy-start | bytes 98308
  24.1 3.8 %collective-permute-start = (bf16[16,128,128]{2,1,0:T(8,128)(2,1)S(1)}, bf16[16,128,128]{2,1,0:T(8,128)(2,1)S(1)}, u32[]{:S(2)}, u32[]{:S(2)}) collective-permute-start(bf16[16,128,128]{2,1,0:T(8,128)(2,1)S(1)} %bitcast.8), channel_id=1, source_target_pairs={{0,16},{1,17},{2,18},{3,19},{4,20},{5,21},{6,22},{7,23},{8,24},{9,... | collective-permute-start | bytes 1572872 | tf_op jit(solution)/shard_map/ppermute | solution.py:43
  27.9 49.5 %copy-start.3 = (bf16[128,128]{1,0:T(8,128)(2,1)S(1)}, bf16[128,128]{1,0:T(8,128)(2,1)}, u32[]{:S(2)}) copy-start(bf16[128,128]{1,0:T(8,128)(2,1)} %weight.1) | copy-start | bytes 98308
  91.0 3.9 %collective-permute-start.1 = (bf16[18,128,128]{2,1,0:T(8,128)(2,1)S(1)}, bf16[18,128,128]{2,1,0:T(8,128)(2,1)S(1)}, u32[]{:S(2)}, u32[]{:S(2)}) collective-permute-start(bf16[18,128,128]{2,1,0:T(8,128)(2,1)S(1)} %get-tuple-element.22), channel_id=1, source_target_pairs={{0,16},{1,17},{2,18},{3,19},{4,20},{5,21},{6,22},{7,23},{8,24},{9,... | collective-permute-start | bytes 1769480 | tf_op jit(solution)/shard_map/ppermute | solution.py:43

commit v10 on v9

--- a/solution.py
+++ b/solution.py
@@ -116,12 +116,13 @@
         x = jnp.where(lax.rem(b, 2) == core_place(), own[spot], other[spot])
         r = rows[t]
         acc[r] += dot(adj[t], x, ((1,), (0,)))
-    out[...] = acc[...].astype(BF).reshape(4, 4, T, F)
+    for k in range(4):
+        out[slot(k)] = acc[pl.ds(4 * k, 4)].astype(BF)
     mine[...] = acc[pl.ds(y_place() * 4, 4)]
 
 
 def add_y(parts, mine, cot, out):
-    out[pl.ds(0, 4)] = plus_others(mine[...], parts, y_place(), 4).astype(BF)
+    out[pl.ds(0, 4)] = plus_others(mine[...], parts, slot(y_place()), 4).astype(BF)
     out[4] = cot[...]
 
 
@@ -214,7 +215,7 @@
         "ssvvv",
         [pltpu.VMEM((16, T, F), F32)],
     )(rows, cols, adj, own, other)
-    parts = exchange(partial, "y")
+    parts = exchange(partial, "y", True)
     (summed,) = call(add_y, [((5, T, F), BF)], "vvv")(parts, mine, cotangent)
     parts = gather(summed, "zh")
     act, back = call(

time: 123 us -> 126 us (1.024)
  the two profiles are of different devices: /device:TPU:6 before, /device:TPU:1 now
where the time goes in v10:
time: 126 us; the launch traced here: 124 us
  blocking collectives  104 us (83%)
  starting transfers between devices  11.8 us (9%)
  Pallas kernels  3.74 us (3%)
  waiting for transfers between devices  3.12 us (2%)
    all_to_all x6, blocking collectives, exchange(): lax.all_to_all(array, BOTH, 0, 0, tiled=True, axis_index_groups=members)  74.2 us
    all_gather x1, blocking collectives, gather(): lax.all_gather(array, BOTH, axis=0, tiled=False, axis_index_groups=groups...  29.4 us
    ppermute x2, starting transfers between devices, swap_core(): return lax.ppermute(array, BOTH, pairs)  11.8 us
    ppermute x2, waiting for transfers between devices, swap_core(): return lax.ppermute(array, BOTH, pairs)  3.12 us
  transfers between devices with their start and end apart: 2, of which 2 were waited for; matrix products, arithmetic and copies ran while one was open for 0% of the time, Pallas kernels for 0%

profile of v10, /device:TPU:1, one launch (start us, length us, event | category | flops | bytes accessed | tf_op | source)
XLA Modules:
  0.0 123.9 jit_solution(7061957824192992483)
XLA Ops:
  0.6 0.0 copy-start
  0.6 0.0 copy-start.1
  0.7 0.8 copy-done.1
  1.5 0.0 copy-start.4
  1.5 0.0 copy-start.5
  1.5 11.0 %all_to_all.30 = bf16[4,128,128]{2,1,0:T(8,128)(2,1)S(1)} all-to-all(bf16[4,128,128]{2,1,0:T(8,128)(2,1)S(1)} %shard_map.85), channel_id=1, replica_groups={{0,32,64,96},{1,33,65,97},{2,34,66,98},{3,35,67,99},{4,36,68,100},{5,37..., dimensions={0} | all-to-all | bytes 262144 | tf_op jit(solution)/shard_map/all_to_all | solution.py:52
  12.5 0.0 copy-start.2
  12.5 0.1 broadcast_in_dim.2
  12.6 10.7 %all_to_all.31 = bf16[4,4,128,128]{3,2,1,0:T(8,128)(2,1)S(1)} all-to-all(bf16[4,4,128,128]{3,2,1,0:T(8,128)(2,1)S(1)} %broadcast_in_dim.2), channel_id=1, replica_groups={{0,128,256,384},{1,129,257,385},{2,130,258,386},{3,131,259,387},{4,132,..., dimensions={0} | all-to-all | bytes 1048576 | tf_op jit(solution)/shard_map/all_to_all | solution.py:52
  23.3 5.8 %collective-permute-start = (bf16[16,128,128]{2,1,0:T(8,128)(2,1)S(1)}, bf16[16,128,128]{2,1,0:T(8,128)(2,1)S(1)}, u32[]{:S(2)}, u32[]{:S(2)}) collective-permute-start(bf16[16,128,128]{2,1,0:T(8,128)(2,1)S(1)} %bitcast.8), channel_id=1, source_target_pairs={{0,16},{1,17},{2,18},{3,19},{4,20},{5,21},{6,22},{7,23},{8,24},{9,... | collective-permute-start | bytes 1572872 | tf_op jit(solution)/shard_map/ppermute | solution.py:43
  29.1 1.5 %collective-permute-done.other = bf16[16,128,128]{2,1,0:T(8,128)(2,1)S(1)} collective-permute-done((bf16[16,128,128]{2,1,0:T(8,128)(2,1)S(1)}, bf16[16,128,128]{2,1,0:T(8,128)(2,1)S(1)}, u32[]{:S(2)}, u32[]{:S(2)}) %collective-permute-start) | collective-permute-done | bytes 524320 | tf_op jit(solution)/shard_map/ppermute | solution.py:43
  30.6 0.0 copy-done
  30.6 0.0 copy-done.4
  30.6 0.0 copy-done.5
  30.6 0.0 copy-start.3
  30.7 1.0 shard_map.86
  31.7 11.1 %all_to_all.32.parts = bf16[4,4,128,128]{3,2,1,0:T(8,128)(2,1)S(1)} all-to-all(bf16[4,4,128,128]{3,2,1,0:T(8,128)(2,1)S(1)} %get-tuple-element.17), channel_id=1, replica_groups={{0,4,8,12},{1,5,9,13},{2,6,10,14},{3,7,11,15},{28,24,20,16},{29,25,21,1..., dimensions={0} | all-to-all | bytes 1048576 | tf_op jit(solution)/shard_map/all_to_all | solution.py:52
  42.8 0.0 copy-done.2
  42.8 0.1 shard_map.87
  42.9 29.4 %all-gather = bf16[20,128,128]{2,1,0:T(8,128)(2,1)S(1)} all-gather(bf16[5,128,128]{2,1,0:T(8,128)(2,1)S(1)} %shard_map.87), channel_id=2, replica_groups={{0,1,2,3},{4,5,6,7},{8,9,10,11},{12,13,14,15},{16,17,18,19},{20,21,22,2..., dimensions={0}, use_global_device_ids=true | all-gather | bytes 819200 | tf_op jit(solution)/shard_map/all_gather | solution.py:47
  72.3 0.0 copy-done.3
  72.3 0.6 shard_map.88
  72.9 16.6 %all_to_all.33.parts = bf16[4,6,128,128]{3,2,1,0:T(8,128)(2,1)S(1)} all-to-all(bf16[4,6,128,128]{3,2,1,0:T(8,128)(2,1)S(1)} %get-tuple-element.19), channel_id=1, replica_groups={{0,4,8,12},{1,5,9,13},{2,6,10,14},{3,7,11,15},{16,20,24,28},{17,21,25,2..., dimensions={0} | all-to-all | bytes 1572864 | tf_op jit(solution)/shard_map/all_to_all | solution.py:52
  89.5 1.1 shard_map.89
  90.5 6.0 %collective-permute-start.1 = (bf16[18,128,128]{2,1,0:T(8,128)(2,1)S(1)}, bf16[18,128,128]{2,1,0:T(8,128)(2,1)S(1)}, u32[]{:S(2)}, u32[]{:S(2)}) collective-permute-start(bf16[18,128,128]{2,1,0:T(8,128)(2,1)S(1)} %get-tuple-element.22), channel_id=1, source_target_pairs={{0,16},{1,17},{2,18},{3,19},{4,20},{5,21},{6,22},{7,23},{8,24},{9,... | collective-permute-start | bytes 1769480 | tf_op jit(solution)/shard_map/ppermute | solution.py:43
  96.6 1.6 %collective-permute-done.1.got = bf16[18,128,128]{2,1,0:T(8,128)(2,1)S(1)} collective-permute-done((bf16[18,128,128]{2,1,0:T(8,128)(2,1)S(1)}, bf16[18,128,128]{2,1,0:T(8,128)(2,1)S(1)}, u32[]{:S(2)}, u32[]{:S(2)}) %collective-permute-start.1) | collective-permute-done | bytes 589856 | tf_op jit(solution)/shard_map/ppermute | solution.py:43
  98.2 0.2 shard_map.90
  98.3 11.9 %all_to_all.34.parts = bf16[4,5,128,128]{3,2,1,0:T(8,128)(2,1)S(1)} all-to-all(bf16[4,5,128,128]{3,2,1,0:T(8,128)(2,1)S(1)} %get-tuple-element.23), channel_id=1, replica_groups={{0,128,256,384},{1,129,257,385},{2,130,258,386},{3,131,259,387},{4,132,..., dimensions={0} | all-to-all | bytes 1310720 | tf_op jit(solution)/shard_map/all_to_all | solution.py:52
  110.2 0.1 shard_map.91
  110.3 12.9 %all_to_all.35.parts = bf16[4,2,128,128]{3,2,1,0:T(8,128)(2,1)S(1)} all-to-all(bf16[4,2,128,128]{3,2,1,0:T(8,128)(2,1)S(1)} %get-tuple-element.25), channel_id=1, replica_groups={{0,32,64,96},{1,33,65,97},{2,34,66,98},{3,35,67,99},{4,36,68,100},{5,37..., dimensions={0} | all-to-all | bytes 524288 | tf_op jit(solution)/shard_map/all_to_all | solution.py:52
  123.2 0.7 shard_map.92
  (1 shorter events, 0.0 us)
Async XLA Ops:
  0.6 30.0 %copy-start = (bf16[1,1,16,128,128]{4,3,2,1,0:T(8,128)(2,1)S(1)}, bf16[1,1,16,128,128]{4,3,2,1,0:T(8,128)(2,1)}, u32[]{:S(2)}) copy-start(bf16[1,1,16,128,128]{4,3,2,1,0:T(8,128)(2,1)} %param.8) | copy-start | bytes 1572868
  0.6 0.8 copy-start.1
  1.5 29.2 %copy-start.4 = (s32[1,1,16]{2,1,0:T(1,128)S(1)}, s32[1,1,16]{2,1,0:T(1,128)}, u32[]{:S(2)}) copy-start(s32[1,1,16]{2,1,0:T(1,128)} %param.9) | copy-start | bytes 196
  1.5 29.2 %copy-start.5 = (s32[1,1,16]{2,1,0:T(1,128)S(1)}, s32[1,1,16]{2,1,0:T(1,128)}, u32[]{:S(2)}) copy-start(s32[1,1,16]{2,1,0:T(1,128)} %param.10) | copy-start | bytes 196
  12.5 30.3 %copy-start.2 = (bf16[128,128]{1,0:T(8,128)(2,1)S(1)}, bf16[128,128]{1,0:T(8,128)(2,1)}, u32[]{:S(2)}) copy-start(bf16[128,128]{1,0:T(8,128)(2,1)} %cot.1) | copy-start | bytes 98308
  23.3 7.3 %collective-permute-start = (bf16[16,128,128]{2,1,0:T(8,128)(2,1)S(1)}, bf16[16,128,128]{2,1,0:T(8,128)(2,1)S(1)}, u32[]{:S(2)}, u32[]{:S(2)}) collective-permute-start(bf16[16,128,128]{2,1,0:T(8,128)(2,1)S(1)} %bitcast.8), channel_id=1, source_target_pairs={{0,16},{1,17},{2,18},{3,19},{4,20},{5,21},{6,22},{7,23},{8,24},{9,... | collective-permute-start | bytes 1572872 | tf_op jit(solution)/shard_map/ppermute | solution.py:43
  30.6 41.6 %copy-start.3 = (bf16[128,128]{1,0:T(8,128)(2,1)S(1)}, bf16[128,128]{1,0:T(8,128)(2,1)}, u32[]{:S(2)}) copy-start(bf16[128,128]{1,0:T(8,128)(2,1)} %weight.1) | copy-start | bytes 98308
  90.5 7.6 %collective-permute-start.1 = (bf16[18,128,128]{2,1,0:T(8,128)(2,1)S(1)}, bf16[18,128,128]{2,1,0:T(8,128)(2,1)S(1)}, u32[]{:S(2)}, u32[]{:S(2)}) collective-permute-start(bf16[18,128,128]{2,1,0:T(8,128)(2,1)S(1)} %get-tuple-element.22), channel_id=1, source_target_pairs={{0,16},{1,17},{2,18},{3,19},{4,20},{5,21},{6,22},{7,23},{8,24},{9,... | collective-permute-start | bytes 1769480 | tf_op jit(solution)/shard_map/ppermute | solution.py:43
